TPU v7x, 256 devices: a whole 4x4x8 slice. The times are simulated.
256 devices in a mesh: wide: 32 (over y, x, core), narrow: 8 (over z).
Axes of the slice: x: 4, y: 4, z: 8, core: 2. Of those that a mesh axis runs over, the one named last changes fastest.
Arguments:
- three_centre: bfloat16 [32, 1024, 4096], P('narrow', 'wide'), may hold values from -6 to 6
- go_blocks: bfloat16 [64, 64, 64], replicated, may hold values from -0.75 to 0.75
- gv_blocks: bfloat16 [64, 64, 64], replicated, may hold values from -0.125 to 0.125
- go_index: int32 [32, 32], P('narrow'), may hold values from 0 to 63
- gv_index: int32 [32, 32], P('narrow'), may hold values from 0 to 63
- source_mask: int32 [32, 32], P('narrow'), may hold values 0 or 1
Outputs:
- chi: float32 [1024, 1024], P('wide', 'narrow')
All inputs are finite; a program needn't handle non-finite values. No bound on the sum of `source_mask` on one device may be relied on, other than what follows from the above.
Results may differ from a plain program's by a relative error of at most 0.004.
Values may be sent and summed in bfloat16 or wider, within the bound.
No kernel may reach another device: no remote copies, remote signals or barrier semaphores. Data moves between devices by JAX's collectives and lax.ppermute only.
A program may use at most 192 MiB of HBM per device.

v0:
```python
import jax
import jax.numpy as jnp
from jax import lax
from jax.sharding import PartitionSpec as P


def local(three_centre, go_blocks, gv_blocks, go_index, gv_index, source_mask):
    local_pairs, aux_local, pair_width = three_centre.shape
    block = go_blocks.shape[1]
    go_chosen = go_blocks[go_index]
    gv_chosen = gv_blocks[gv_index] * source_mask.astype(jnp.bfloat16)[:, :, None, None]
    piece = lax.all_gather(three_centre, "narrow", axis=0, tiled=True)
    number_sources = piece.shape[0]
    sources = piece.reshape(number_sources, aux_local, block, block)
    results = []
    for target in range(local_pairs):
        first_product = jnp.einsum(
            "cma,cpmn->cpan", go_chosen[target], sources, preferred_element_type=jnp.float32
        ).astype(jnp.bfloat16)
        results.append(
            jnp.einsum(
                "cpan,cnd->pad",
                first_product,
                gv_chosen[target],
                preferred_element_type=jnp.float32,
            )
        )
    summed = jnp.stack(results)
    image = summed.reshape(local_pairs, aux_local, pair_width).astype(jnp.bfloat16)
    norm_scale = 1.0 / jnp.sqrt(jnp.float32(local_pairs * lax.axis_size("narrow") * pair_width))
    partial_chi = jnp.einsum(
        "kpe,kqe->pq",
        image,
        lax.all_gather(three_centre, "wide", axis=1, tiled=True),
        preferred_element_type=jnp.float32,
    )
    result = lax.psum_scatter(partial_chi, "narrow", scatter_dimension=1, tiled=True)
    return result * norm_scale


def solution(mesh):
    placed = (
        P("narrow", "wide", None),
        P(),
        P(),
        P("narrow", None),
        P("narrow", None),
        P("narrow", None),
    )
    return jax.shard_map(
        local, mesh=mesh, in_specs=placed, out_specs=P("wide", "narrow"), check_vma=False
    )
```

profile of v0, /device:TPU:16, one launch (start us, length us, event | category | flops | bytes accessed | tf_op | source)
XLA Modules:
  0.0 286.1 jit_solution(9310431331818708807)
XLA Ops:
  6.5 0.7 all-gather.3.cloned.1.call-update
  7.3 0.7 all-gather.5.cloned.1.call-update
  8.1 0.7 compare_select_fusion
  8.7 0.1 reshape.28
  8.8 0.7 convert_element_type.30
  9.5 0.7 compare_select_fusion.1
  10.2 0.1 reshape.20
  10.3 1.0 gather_fusion.1
  11.3 3.4 %gather_fusion = bf16[128,64,64]{2,1,0:T(8,128)(2,1)} fusion(bf16[64,64,64]{2,1,0:T(8,128)(2,1)} %param.7, s32[1024]{0:T(1024)S(1)} %pad_clamp_fusion.1), kind=kCustom, calls=%fused_computation | custom fusion | bytes 2097664 | tf_op jit(solution)/shard_map/gather | solution.py:10
  14.7 1.5 broadcast_multiply_fusion
  16.2 89.9 %all-gather.3.cloned.1.call-done = bf16[32,32,4096]{2,1,0:T(8,128)(2,1)} async-done(((bf16[4,32,4096]{2,1,0:T(8,128)(2,1)}), bf16[32,32,4096]{2,1,0:T(8,128)(2,1)}) %all-gather.3.cloned.1.call-update) | async-done | bytes 8388624 | tf_op jit(solution)/shard_map/all_gather | solution.py:12
  106.1 23.6 %reshape.17 = bf16[32,32,64,64]{3,2,1,0:T(8,128)(2,1)} reshape(bf16[32,32,4096]{2,1,0:T(8,128)(2,1)} %all-gather.3.cloned.1.call-done) | data formatting | bytes 16777216 | tf_op jit(solution)/shard_map/reshape | solution.py:14
  129.7 10.8 %fusion.63 = bf16[32,64,64]{2,1,0:T(8,128)(2,1)S(1)} fusion(bf16[32,32,64,64]{3,2,1,0:T(8,128)(2,1)} %reshape.17, bf16[4,32,64,64]{3,2,1,0:T(8,128)(2,1)S(1)} %copy-done.2, bf16[128,64,64]{2,1,0:T(8,128)(2,1)} %gather_fusion), kind=kOutput, calls=%fused_computation.29 | convolution fusion | flops 1078067200 | bytes 18087936 | tf_op jit(solution)/shard_map/cpan,cnd->pad/dot_general | solution.py:21
  140.5 0.5 stack.15
  141.0 10.6 %fusion.58 = bf16[32,64,64]{2,1,0:T(8,128)(2,1)S(1)} fusion(bf16[32,32,64,64]{3,2,1,0:T(8,128)(2,1)} %reshape.17, bf16[4,32,64,64]{3,2,1,0:T(8,128)(2,1)S(1)} %copy-done.2, bf16[128,64,64]{2,1,0:T(8,128)(2,1)} %gather_fusion), kind=kOutput, calls=%fused_computation.28 | convolution fusion | flops 1078067200 | bytes 18087936 | tf_op jit(solution)/shard_map/cpan,cnd->pad/dot_general | solution.py:21
  151.6 1.2 stack.16
  152.7 12.7 %fusion.53 = bf16[32,64,64]{2,1,0:T(8,128)(2,1)S(1)} fusion(bf16[32,32,64,64]{3,2,1,0:T(8,128)(2,1)} %reshape.17, bf16[4,32,64,64]{3,2,1,0:T(8,128)(2,1)S(1)} %copy-done.2, bf16[128,64,64]{2,1,0:T(8,128)(2,1)} %gather_fusion), kind=kOutput, calls=%fused_computation.27 | convolution fusion | flops 1078067200 | bytes 18087936 | tf_op jit(solution)/shard_map/cpan,cnd->pad/dot_general | solution.py:21
  165.4 1.2 stack.17
  166.6 11.7 %fusion.48 = bf16[32,64,64]{2,1,0:T(8,128)(2,1)} fusion(bf16[32,32,64,64]{3,2,1,0:T(8,128)(2,1)} %reshape.17, bf16[4,32,64,64]{3,2,1,0:T(8,128)(2,1)S(1)} %copy-done.2, bf16[128,64,64]{2,1,0:T(8,128)(2,1)} %gather_fusion), kind=kOutput, calls=%fused_computation.26 | convolution fusion | flops 1078067200 | bytes 18087936 | tf_op jit(solution)/shard_map/cpan,cnd->pad/dot_general | solution.py:21
  178.3 1.6 stack.18
  179.9 45.5 %all-gather.5.cloned.1.call-done = bf16[4,1024,4096]{2,1,0:T(8,128)(2,1)} async-done(((bf16[4,32,4096]{2,1,0:T(8,128)(2,1)}), bf16[4,1024,4096]{2,1,0:T(8,128)(2,1)}) %all-gather.5.cloned.1.call-update) | async-done | bytes 33554448 | tf_op jit(solution)/shard_map/all_gather | solution.py:34
  225.4 16.0 %convolution_bitcast_fusion = f32[32,1024]{1,0:T(8,128)} fusion(bf16[4,1024,4096]{2,1,0:T(8,128)(2,1)} %all-gather.5.cloned.1.call-done, bf16[1,32,4096]{2,1,0:T(8,128)(2,1)S(1)} %stack.18, bf16[1,32,4096]{2,1,0:T(8,128)(2,1)} %stack.17, bf16[1,32,4096]{2,1,0:T(8,128)(2,1)} %stack.16, bf16[1,32,4096]{2,1,0:T(8,128)(2,1)S(1)} %stack.15), kind=kOutput, calls=%fused_computation.30 | convolution fusion | flops 1075314688 | bytes 34734080 | tf_op jit(solution)/shard_map/kpe,kqe->pq/dot_general | solution.py:31
  241.4 36.8 %reduce-scatter.2.cloned.1.call-done = f32[32,128]{1,0:T(8,128)} async-done(((f32[32,1024]{1,0:T(8,128)}), f32[32,128]{1,0:T(8,128)}) %reduce-scatter.2.cloned.1.call-update) | async-done | bytes 16400 | tf_op jit(solution)/shard_map/reduce_scatter | solution.py:37
  278.3 1.3 broadcast_multiply_fusion.1
  (12 shorter events, 0.1 us)
Async XLA Ops:
  6.5 3.8 %copy-start = (bf16[64,64,64]{2,1,0:T(8,128)(2,1)S(1)}, bf16[64,64,64]{2,1,0:T(8,128)(2,1)}, u32[]{:S(2)}) copy-start(bf16[64,64,64]{2,1,0:T(8,128)(2,1)} %param.8) | copy-start | bytes 1572868
  6.5 99.6 %all-gather.3.cloned.1.call-start = ((), (), s32[]{:S(2)}) async-start(), calls=%async_computation.1 | async-start | bytes 9437184 | tf_op jit(solution)/shard_map/all_gather | solution.py:12
  7.3 218.1 %all-gather.5.cloned.1.call-start = ((), (), s32[]{:S(2)}) async-start(), calls=%async_computation.2 | async-start | bytes 34603008 | tf_op jit(solution)/shard_map/all_gather | solution.py:34
  8.0 270.3 %reduce-scatter.2.cloned.1.call-start = ((), (), s32[]{:S(2)}) async-start(), calls=%async_computation.3 | async-start | bytes 147456 | tf_op jit(solution)/shard_map/reduce_scatter | solution.py:37
  16.2 113.6 %copy-start.2 = (bf16[4,32,64,64]{3,2,1,0:T(8,128)(2,1)S(1)}, bf16[4,32,64,64]{3,2,1,0:T(8,128)(2,1)}, u32[]{:S(2)}) copy-start(bf16[4,32,64,64]{3,2,1,0:T(8,128)(2,1)} %broadcast_multiply_fusion) | copy-start | bytes 3145732
  178.3 101.3 %copy-start.1 = (bf16[64,64,64]{2,1,0:T(8,128)(2,1)S(1)}, bf16[64,64,64]{2,1,0:T(8,128)(2,1)}, u32[]{:S(2)}) copy-start(bf16[64,64,64]{2,1,0:T(8,128)(2,1)} %param.8) | copy-start | bytes 1572868
Sparse Core Ops, SparseCore 0:
  9.1 96.9 all-gather.2
  108.7 116.6 all-gather.4
  241.5 36.6 reduce-scatter.1
where the time goes:
time: 287 us; the launch traced here: 286 us
  waiting for transfers between devices  174 us (61%)
  matrix products  61.7 us (21%)
  local copies, waits for them, and re-layouts  32.5 us (11%)
  between operations  13.2 us (5%)
  other arithmetic  4.92 us (2%)
    all_gather x1, waiting for transfers between devices, local(): piece = lax.all_gather(three_centre, 'narrow', axis=0, tiled=True)  89.9 us
    dot_general x4, matrix products, local(): jnp.einsum('cpan,cnd->pad', first_product, gv_chosen[target], preferred_e...  45.7 us
    all_gather x1, waiting for transfers between devices, local(): lax.all_gather(three_centre, 'wide', axis=1, tiled=True)  45.5 us
    reduce_scatter x1, waiting for transfers between devices, local(): lax.psum_scatter(partial_chi, 'narrow', scatter_dimension=1, tiled=True)  36.8 us
    reshape x1, local copies, waits for them, and re-layouts, local(): sources = piece.reshape(number_sources, aux_local, block, block)  23.6 us
    dot_general x1, matrix products, local(): jnp.einsum('kpe,kqe->pq', image, lax.all_gather(three_centre, 'wide', axi...  16 us
  transfers between devices with their start and end apart: 3, of which 3 were waited for; matrix products, arithmetic and copies ran while one was open for 29% of the time, Pallas kernels for 0%

commit v1 on v0

v1 whole, which is shorter than its diff:
```python
import functools

import jax
import jax.numpy as jnp
from jax import lax
from jax.experimental import pallas as pl
from jax.experimental.pallas import tpu as pltpu
from jax.sharding import Mesh, PartitionSpec as P

WIDE = ("y", "x", "core")
LANES = 128
BLK = 64
VMEM = pltpu.VMEM
SMEM = pltpu.SMEM


def vmem(n):
    return [pl.BlockSpec(memory_space=VMEM)] * n


def pair_halves(first, second):
    left = lax.broadcasted_iota(jnp.int32, first.shape, 1) < BLK
    low = jnp.where(left, first, pltpu.roll(second, BLK, 1))
    high = jnp.where(left, pltpu.roll(first, BLK, 1), second)
    return low, high


def spread_kernel(c_ref, code_ref, out_ref):
    pairs, aux, width = c_ref.shape
    half = width // LANES
    for j in range(pairs):
        for g in range(aux // 16):
            x = c_ref[j, 16 * g : 16 * g + 16, :].astype(jnp.float32)
            x = pltpu.einshape("p(tl)->ptl", x, l=LANES)
            for i in range(4):
                low01, high01 = pair_halves(x[4 * i], x[4 * i + 1])
                low23, high23 = pair_halves(x[4 * i + 2], x[4 * i + 3])
                d = 4 * g + i
                r = 2 * half * j
                out_ref[d, r : r + half, :LANES] = low01.astype(jnp.bfloat16)
                out_ref[d, r : r + half, LANES:] = low23.astype(jnp.bfloat16)
                out_ref[d, r + half : r + 2 * half, :LANES] = high01.astype(jnp.bfloat16)
                out_ref[d, r + half : r + 2 * half, LANES:] = high23.astype(jnp.bfloat16)
    rows = pairs * 2 * half
    for d in range(aux // 4):
        out_ref[d, rows : rows + 16, :] = code_ref[...]


def image_kernel(go_code, gv_code, w_ref, gt_ref, vb_ref, out_ref, stage):
    nsrc = w_ref.shape[0]
    pairs = 4
    number = nsrc * pairs
    step = 8

    @pl.loop(0, nsrc)
    def _(zd):
        for kk in range(pairs):
            k = zd * pairs + kk
            acc = None
            for jb in range(0, number, step):
                lefts, rights = [], []
                for j in range(jb, jb + step):
                    g = go_code[k, j]
                    v = gv_code[k, j]
                    r = BLK * (j % pairs)
                    first = jnp.dot(
                        gt_ref[g], w_ref[j // pairs, r : r + BLK, :], preferred_element_type=jnp.float32
                    ).astype(jnp.bfloat16)
                    lefts.append(jnp.concatenate([first[:, :LANES], first[:, LANES:]], axis=0))
                    rights.append(vb_ref[v])
                part = jnp.dot(
                    jnp.concatenate(lefts, axis=1),
                    jnp.concatenate(rights, axis=0),
                    preferred_element_type=jnp.float32,
                )
                acc = part if acc is None else acc + part
            for h in range(2):
                even, odd = acc[BLK * h : BLK * h + 32], acc[BLK * h + 32 : BLK * h + 64]
                p0, p1 = pair_halves(even, odd)
                stage[4 * kk + 2 * h] = p0
                stage[4 * kk + 2 * h + 1] = p1
        y = pltpu.einshape("ptl->p(tl)", stage[...]).astype(jnp.bfloat16)
        width = out_ref.shape[3]
        for xd in range(out_ref.shape[0]):
            out_ref[xd, zd] = y[:, width * xd : width * xd + width]


def chi_kernel(scale, ypos, im_ref, *refs):
    pieces, out_ref = refs[:-1], refs[-1]
    shifts = (0, 1, 3, 2)
    for s in range(4):
        own, other = pieces[2 * s], pieces[2 * s + 1]
        acc = None
        for k in range(4):
            rhs = jnp.concatenate(
                [ref[x, k] for x in range(4) for ref in (own, other)], axis=0
            )
            part = lax.dot_general(
                im_ref[k], rhs, (((1,), (1,)), ((), ())), preferred_element_type=jnp.float32
            )
            acc = part if acc is None else acc + part
        acc = (acc * scale).astype(jnp.bfloat16)
        y = lax.rem(ypos[0] + 4 - shifts[s], 4)
        for xd in range(4):
            for h in range(2):
                out_ref[xd, 2 * y + h] = acc[32 * xd : 32 * xd + 32, LANES * h : LANES * h + LANES]


def local(three_centre, go_blocks, gv_blocks, go_index, gv_index, source_mask):
    pairs, aux, width = three_centre.shape
    nz = lax.axis_size("z")
    nx = lax.axis_size("x")
    number = pairs * nz
    blocks = go_blocks.shape[0]
    scale = float((number * width) ** -0.5)

    codes = jnp.concatenate([go_index, jnp.where(source_mask != 0, gv_index, blocks)], axis=0)
    codes = jnp.broadcast_to(codes.astype(jnp.bfloat16).reshape(1, 2 * pairs * number), (16, 2 * pairs * number))
    rows = pairs * BLK
    spread = pl.pallas_call(
        spread_kernel,
        out_shape=jax.ShapeDtypeStruct((nz, rows + 16, 4 * BLK), jnp.bfloat16),
        in_specs=vmem(2),
        out_specs=vmem(1)[0],
        name="spread",
    )(three_centre, codes)
    w = lax.all_to_all(spread, "z", 0, 0, tiled=True)

    cx = three_centre.reshape(pairs, aux, nx, width // nx).transpose(2, 0, 1, 3)
    cx = lax.all_to_all(cx, "x", 0, 0, tiled=True)
    swap = [(0, 1), (1, 0)]
    pieces = []
    for s in (0, 1, 3, 2):
        own = cx if s == 0 else lax.ppermute(cx, "y", [(i, (i + s) % 4) for i in range(4)])
        pieces += [own, lax.ppermute(own, "core", swap)]

    gt = go_blocks.reshape(blocks, 32, 2, 32, 2).transpose(0, 4, 3, 2, 1).reshape(blocks, BLK, BLK)
    zero = jnp.zeros_like(gv_blocks)
    vb = jnp.concatenate(
        [jnp.concatenate([gv_blocks, zero], axis=2), jnp.concatenate([zero, gv_blocks], axis=2)], axis=1
    )
    vb = jnp.concatenate([vb, jnp.zeros((1, LANES, LANES), jnp.bfloat16)], axis=0)

    got = w[:, rows, :].astype(jnp.int32).reshape(nz, 2, pairs, number)
    go_code = got[:, 0].reshape(number, number)
    gv_code = got[:, 1].reshape(number, number)
    image = pl.pallas_call(
        image_kernel,
        out_shape=jax.ShapeDtypeStruct((nx, nz, 4 * pairs, width // nx), jnp.bfloat16),
        in_specs=[pl.BlockSpec(memory_space=SMEM)] * 2 + vmem(3),
        out_specs=vmem(1)[0],
        scratch_shapes=[VMEM((4 * pairs, width // LANES, LANES), jnp.float32)],
        name="image",
    )(go_code, gv_code, w, gt, vb)
    image = lax.all_to_all(image.reshape(nx * nz, 4 * pairs, width // nx), ("x", "z"), 0, 0, tiled=True)
    image = image.reshape(nx * nz, pairs, 4, width // nx).transpose(1, 0, 2, 3)
    image = image.reshape(pairs, nx * nz * 4, width // nx)

    part = pl.pallas_call(
        functools.partial(chi_kernel, scale),
        out_shape=jax.ShapeDtypeStruct((nx, nz, aux, 4 * aux), jnp.bfloat16),
        in_specs=[pl.BlockSpec(memory_space=SMEM)] + vmem(9),
        out_specs=vmem(1)[0],
        name="chi",
    )(lax.axis_index("y").reshape(1), image, *pieces)
    part = lax.all_to_all(part.reshape(nx * nz, aux, 4 * aux), ("x", "z"), 0, 0, tiled=True)
    chi = jnp.sum(part.astype(jnp.float32), axis=0).reshape(aux, 2, 2, aux)
    chi = jnp.where(lax.axis_index("core") == 0, chi, chi[:, :, ::-1])
    return chi.reshape(aux, 4 * aux)


def solution(mesh):
    grid = Mesh(mesh.devices.reshape(4, 4, 2, 8), WIDE + ("z",))
    rows = P("z", None)
    return jax.shard_map(
        local,
        mesh=grid,
        in_specs=(P("z", WIDE, None), P(), P(), rows, rows, rows),
        out_specs=P(WIDE, "z"),
        check_vma=False,
    )
```

time: 287 us -> 152 us (0.53)
  waiting for transfers between devices: 174 us -> 66.4 us
  matrix products: 61.7 us -> 0 us
  Pallas kernels: 0 us -> 41 us
  starting transfers between devices: 0.08 us -> 26.4 us
  local copies, waits for them, and re-layouts: 32.5 us -> 15.5 us
  between operations: 13.2 us -> 0.17 us
    all_gather x2 -> x0, waiting for transfers between devices: 135 us -> none  [the longest x1 89.9 us: local(): piece = lax.all_gather(three_centre, 'narrow', axis=0, tiled=True)]
    all_to_all x0 -> x4, waiting for transfers between devices: none -> 66.3 us  [the longest x1 27.9 us: local(): lax.all_to_all(image.reshape(nx * nz, 4 * pairs, width // nx), ('x', 'z')...]
    dot_general x5 -> x0, matrix products: 61.7 us -> none  [the longest x4 45.7 us: local(): jnp.einsum('cpan,cnd->pad', first_product, gv_chosen[target], preferred_e...]
    pallas_call x0 -> x3, Pallas kernels: none -> 41 us  [the longest x1 30.6 us: local(): pl.pallas_call(image_kernel, out_shape=jax.ShapeDtypeStruct((nx, nz, 4 *...]
    reduce_scatter x1 -> x0, waiting for transfers between devices: 36.8 us -> none  [local(): lax.psum_scatter(partial_chi, 'narrow', scatter_dimension=1, tiled=True)]
    all_to_all x0 -> x4, starting transfers between devices: none -> 21.8 us  [the longest x1 8.47 us: local(): w = lax.all_to_all(spread, 'z', 0, 0, tiled=True)]
    reshape x1 -> x5, local copies, waits for them, and re-layouts: 23.6 us -> 6.72 us  [the longest x1 2.36 us: local(): go_blocks.reshape(blocks, 32, 2, 32, 2).transpose(0, 4, 3, 2, 1)]
    ppermute x0 -> x7, starting transfers between devices: none -> 4.66 us  [the longest x3 3.57 us: local(): lax.ppermute(cx, 'y', [(i, (i + s) % 4) for i in range(4)])]
  transfers between devices with their start and end apart: 3 -> 11, of which waited for: 3 -> 4; matrix products, arithmetic and copies ran while one was open for 29% -> 9% of each run, Pallas kernels for 0% -> 22%
where the time goes in v1:
time: 152 us
  waiting for transfers between devices  66.4 us (44%)
  Pallas kernels  41 us (27%)
  starting transfers between devices  26.4 us (17%)
  local copies, waits for them, and re-layouts  15.5 us (10%)
  other arithmetic  2.46 us (2%)
    pallas_call x1, Pallas kernels, local(): pl.pallas_call(image_kernel, out_shape=jax.ShapeDtypeStruct((nx, nz, 4 *...  30.6 us
    all_to_all x1, waiting for transfers between devices, local(): lax.all_to_all(image.reshape(nx * nz, 4 * pairs, width // nx), ('x', 'z')...  27.9 us
    all_to_all x1, waiting for transfers between devices, local(): w = lax.all_to_all(spread, 'z', 0, 0, tiled=True)  15.2 us
    all_to_all x1, waiting for transfers between devices, local(): lax.all_to_all(part.reshape(nx * nz, aux, 4 * aux), ('x', 'z'), 0, 0, til...  12 us
    all_to_all x1, waiting for transfers between devices, local(): cx = lax.all_to_all(cx, 'x', 0, 0, tiled=True)  11.3 us
    all_to_all x1, starting transfers between devices, local(): w = lax.all_to_all(spread, 'z', 0, 0, tiled=True)  8.47 us
    pallas_call x1, Pallas kernels, local(): pl.pallas_call(functools.partial(chi_kernel, scale), out_shape=jax.ShapeD...  7.31 us
    all_to_all x1, starting transfers between devices, local(): lax.all_to_all(part.reshape(nx * nz, aux, 4 * aux), ('x', 'z'), 0, 0, til...  5.08 us
  transfers between devices with their start and end apart: 11, of which 4 were waited for; matrix products, arithmetic and copies ran while one was open for 9% of the time, Pallas kernels for 22%

profile of v1, /device:TPU:16, one launch (start us, length us, event | category | flops | bytes accessed | tf_op | source)
XLA Modules:
  0.0 151.9 jit_solution(5005001722430438525)
XLA Ops:
  0.0 2.3 %copy.22 = bf16[4,4,4,8,1024]{4,3,1,0,2:T(8,128)(2,1)} copy(bf16[4,4,4,8,1024]{4,3,2,1,0:T(8,128)(2,1)} %bitcast.19) | data formatting | bytes 2097152 | tf_op jit(solution)/shard_map/reshape | solution.py:129
  2.4 4.3 %all-to-all-start.2 = ((bf16[4,4,32,1024]{3,2,1,0:T(8,128)(2,1)}), bf16[4,4,32,1024]{3,2,1,0:T(8,128)(2,1)S(1)}, u32[]{:S(2)}, u32[]{:S(2)}) async-start(bf16[4,4,32,1024]{3,2,1,0:T(8,128)(2,1)} %bitcast.18), calls=%async_computation.2 | async-start | bytes 2097152 | tf_op jit(solution)/shard_map/all_to_all | solution.py:130
  7.4 3.1 %spread.1 = bf16[8,272,256]{2,1,0:T(8,128)(2,1)} custom-call(bf16[4,32,4096]{2,1,0:T(8,128)(2,1)} %c_ref.1, bf16[16,256]{1,0:T(8,128)(2,1)} %broadcast_in_dim.12.code_ref), custom_call_target="tpu_custom_call" | custom-call | tf_op jit(solution)/shard_map/spread/pallas_call | solution.py:120
  10.5 11.3 %all-to-all-done.2.refs_0_ = bf16[4,4,32,1024]{3,2,1,0:T(8,128)(2,1)S(1)} async-done(((bf16[4,4,32,1024]{3,2,1,0:T(8,128)(2,1)}), bf16[4,4,32,1024]{3,2,1,0:T(8,128)(2,1)S(1)}, u32[]{:S(2)}, u32[]{:S(2)}) %all-to-all-start.2) | async-done | bytes 1048608 | tf_op jit(solution)/shard_map/all_to_all | solution.py:130
  21.7 8.5 %all-to-all-start = ((bf16[8,272,256]{2,1,0:T(8,128)(2,1)}), bf16[8,272,256]{2,1,0:T(8,128)(2,1)S(1)}, u32[]{:S(2)}, u32[]{:S(2)}) async-start(bf16[8,272,256]{2,1,0:T(8,128)(2,1)} %spread.1), calls=%async_computation | async-start | bytes 2228224 | tf_op jit(solution)/shard_map/all_to_all | solution.py:127
  30.2 2.0 %copy.14 = bf16[64,64,64]{0,2,1:T(8,128)(2,1)} copy(bf16[64,64,64]{2,1,0:T(8,128)(2,1)S(1)} %copy-done.3) | data formatting | bytes 1048576 | tf_op args[1]
  32.2 1.9 %copy.15 = bf16[64,2,32,2,32]{0,4,3,2,1:T(8,128)(2,1)S(1)} copy(bf16[64,2,32,2,32]{0,1,2,3,4:T(2,128)(2,1)} %bitcast.22) | data formatting | bytes 1048576 | tf_op jit(solution)/shard_map/transpose | solution.py:137
  34.1 2.4 %copy.16.gt_ref = bf16[64,64,64]{2,1,0:T(8,128)(2,1)} copy(bf16[64,64,64]{0,2,1:T(8,128)(2,1)S(1)} %bitcast.20) | data formatting | bytes 1048576 | tf_op jit(solution)/shard_map/reshape | solution.py:137
  36.5 2.3 %fusion.2 = bf16[64,128,128]{2,1,0:T(8,128)(2,1)S(1)} fusion(bf16[64,64,64]{2,1,0:T(8,128)(2,1)} %param.8), kind=kLoop, calls=%fused_computation.4 | loop fusion | flops 8388608 | bytes 2621440 | tf_op jit(solution)/shard_map/concatenate | solution.py:139
  38.8 1.6 %concatenate.20.vb_ref = bf16[65,128,128]{2,1,0:T(8,128)(2,1)} pad(bf16[64,128,128]{2,1,0:T(8,128)(2,1)S(1)} %fusion.2, bf16[]{:T(256)} %constant.6.clone.1), padding=0_1x0_0x0_0 | pad | bytes 4227074 | tf_op jit(solution)/shard_map/concatenate | solution.py:142
  40.4 1.3 collective-permute-start.1
  41.7 0.7 collective-permute-start.3
  42.4 1.5 %collective-permute-start.5 = (bf16[4,4,32,1024]{3,2,1,0:T(8,128)(2,1)S(1)}, bf16[4,4,32,1024]{3,2,1,0:T(8,128)(2,1)}, u32[]{:S(2)}, u32[]{:S(2)}) collective-permute-start(bf16[4,4,32,1024]{3,2,1,0:T(8,128)(2,1)S(1)} %all-to-all-done.2.refs_0_), channel_id=1, source_target_pairs={{0,128},{64,192},{128,0},{192,64},{1,129},{65,193},{129,1},{193,65... | collective-permute-start | bytes 3145736 | tf_op jit(solution)/shard_map/ppermute | solution.py:134
  44.0 15.2 %all-to-all-done.w_ref = bf16[8,272,256]{2,1,0:T(8,128)(2,1)S(1)} async-done(((bf16[8,272,256]{2,1,0:T(8,128)(2,1)}), bf16[8,272,256]{2,1,0:T(8,128)(2,1)S(1)}, u32[]{:S(2)}, u32[]{:S(2)}) %all-to-all-start) | async-done | bytes 1114144 | tf_op jit(solution)/shard_map/all_to_all | solution.py:127
  59.3 0.8 fusion.4
  60.2 30.6 %image.1 = bf16[4,8,16,1024]{3,2,1,0:T(8,128)(2,1)} custom-call(s32[32,32]{1,0:T(8,128)} %bitcast.26, s32[32,32]{1,0:T(8,128)} %bitcast.25, bf16[8,272,256]{2,1,0:T(8,128)(2,1)} %copy-done, bf16[64,64,64]{2,1,0:T(8,128)(2,1)} %copy.16.gt_ref, bf16[65,128,128]{2,1,0:T(8,128)(2,1)} %concatenate.20.vb_ref), custom_call_target="tpu_custom_call" | custom-call | tf_op jit(solution)/shard_map/image/pallas_call | solution.py:147
  90.8 3.9 %all-to-all-start.1 = ((bf16[32,16,1024]{2,1,0:T(8,128)(2,1)}), bf16[32,16,1024]{2,1,0:T(8,128)(2,1)S(1)}, u32[]{:S(2)}, u32[]{:S(2)}) async-start(bf16[32,16,1024]{2,1,0:T(8,128)(2,1)} %bitcast.23), calls=%async_computation.1 | async-start | bytes 2097152 | tf_op jit(solution)/shard_map/all_to_all | solution.py:155
  95.9 27.9 %all-to-all-done.1 = bf16[32,16,1024]{2,1,0:T(8,128)(2,1)S(1)} async-done(((bf16[32,16,1024]{2,1,0:T(8,128)(2,1)}), bf16[32,16,1024]{2,1,0:T(8,128)(2,1)S(1)}, u32[]{:S(2)}, u32[]{:S(2)}) %all-to-all-start.1) | async-done | bytes 1048608 | tf_op jit(solution)/shard_map/all_to_all | solution.py:155
  124.4 0.8 copy.18
  125.2 1.2 reshape.46.im_ref
  126.4 7.3 %chi.1 = bf16[4,8,32,128]{3,2,1,0:T(8,128)(2,1)} custom-call(s32[1]{0:T(128)} %bitcast.ypos, bf16[4,128,1024]{2,1,0:T(8,128)(2,1)} %reshape.46.im_ref, bf16[4,4,32,1024]{3,2,1,0:T(8,128)(2,1)} %copy-done.1, bf16[4,4,32,1024]{3,2,1,0:T(8,128)(2,1)} %collective-permute-done.refs_1_, bf16[4,4,32,1024]{3,2,1,0:T(8,128)(2,1)} %copy-done.2, ...), custom_call_target="tpu_custom_call" | custom-call | tf_op jit(solution)/shard_map/chi/pallas_call | solution.py:159
  133.8 5.1 %all-to-all-start.3 = ((bf16[32,32,128]{2,1,0:T(8,128)(2,1)}), bf16[32,32,128]{2,1,0:T(8,128)(2,1)S(1)}, u32[]{:S(2)}, u32[]{:S(2)}) async-start(bf16[32,32,128]{2,1,0:T(8,128)(2,1)} %bitcast.24), calls=%async_computation.3 | async-start | bytes 524288 | tf_op jit(solution)/shard_map/all_to_all | solution.py:166
  138.9 12.0 %all-to-all-done.3 = bf16[32,32,128]{2,1,0:T(8,128)(2,1)S(1)} async-done(((bf16[32,32,128]{2,1,0:T(8,128)(2,1)}), bf16[32,32,128]{2,1,0:T(8,128)(2,1)S(1)}, u32[]{:S(2)}, u32[]{:S(2)}) %all-to-all-start.3) | async-done | bytes 262176 | tf_op jit(solution)/shard_map/all_to_all | solution.py:166
  151.2 0.7 reshape.50
  (37 shorter events, 3.0 us)
Async XLA Ops:
  0.0 6.6 %copy-start.4 = (s32[4,32]{1,0:T(4,128)S(1)}, s32[4,32]{1,0:T(4,128)}, u32[]{:S(2)}) copy-start(s32[4,32]{1,0:T(4,128)} %param.9) | copy-start | bytes 1540
  0.0 6.7 %copy-start.5 = (s32[4,32]{1,0:T(4,128)S(1)}, s32[4,32]{1,0:T(4,128)}, u32[]{:S(2)}) copy-start(s32[4,32]{1,0:T(4,128)} %param.10) | copy-start | bytes 1540
  0.0 6.7 %copy-start.6 = (s32[4,32]{1,0:T(4,128)S(1)}, s32[4,32]{1,0:T(4,128)}, u32[]{:S(2)}) copy-start(s32[4,32]{1,0:T(4,128)} %param.11) | copy-start | bytes 1540
  2.4 19.4 %all-to-all-start.2 = ((bf16[4,4,32,1024]{3,2,1,0:T(8,128)(2,1)}), bf16[4,4,32,1024]{3,2,1,0:T(8,128)(2,1)S(1)}, u32[]{:S(2)}, u32[]{:S(2)}) async-start(bf16[4,4,32,1024]{3,2,1,0:T(8,128)(2,1)} %bitcast.18), calls=%async_computation.2 | async-start | bytes 2097152 | tf_op jit(solution)/shard_map/all_to_all | solution.py:130
  7.4 22.8 %copy-start.3 = (bf16[64,64,64]{2,1,0:T(8,128)(2,1)S(1)}, bf16[64,64,64]{2,1,0:T(8,128)(2,1)}, u32[]{:S(2)}) copy-start(bf16[64,64,64]{2,1,0:T(8,128)(2,1)} %param.7) | copy-start | bytes 1572868
  21.7 73.0 %copy-start.1 = (bf16[4,4,32,1024]{3,2,1,0:T(8,128)(2,1)}, bf16[4,4,32,1024]{3,2,1,0:T(8,128)(2,1)S(1)}, u32[]{:S(2)}) copy-start(bf16[4,4,32,1024]{3,2,1,0:T(8,128)(2,1)S(1)} %all-to-all-done.2.refs_0_) | copy-start | bytes 3145732
  21.7 37.4 %all-to-all-start = ((bf16[8,272,256]{2,1,0:T(8,128)(2,1)}), bf16[8,272,256]{2,1,0:T(8,128)(2,1)S(1)}, u32[]{:S(2)}, u32[]{:S(2)}) async-start(bf16[8,272,256]{2,1,0:T(8,128)(2,1)} %spread.1), calls=%async_computation | async-start | bytes 2228224 | tf_op jit(solution)/shard_map/all_to_all | solution.py:127
  40.4 54.4 %collective-permute-start.1 = (bf16[4,4,32,1024]{3,2,1,0:T(8,128)(2,1)S(1)}, bf16[4,4,32,1024]{3,2,1,0:T(8,128)(2,1)S(1)}, u32[]{:S(2)}, u32[]{:S(2)}) collective-permute-start(bf16[4,4,32,1024]{3,2,1,0:T(8,128)(2,1)S(1)} %all-to-all-done.2.refs_0_), channel_id=1, source_target_pairs={{0,64},{64,128},{128,192},{192,0},{1,65},{65,129},{129,193},{193,1... | collective-permute-start | bytes 3145736 | tf_op jit(solution)/shard_map/ppermute | solution.py:134
  41.7 53.7 %collective-permute-start.3 = (bf16[4,4,32,1024]{3,2,1,0:T(8,128)(2,1)S(1)}, bf16[4,4,32,1024]{3,2,1,0:T(8,128)(2,1)}, u32[]{:S(2)}, u32[]{:S(2)}) collective-permute-start(bf16[4,4,32,1024]{3,2,1,0:T(8,128)(2,1)S(1)} %all-to-all-done.2.refs_0_), channel_id=1, source_target_pairs={{0,192},{64,0},{128,64},{192,128},{1,193},{65,1},{129,65},{193,129... | collective-permute-start | bytes 3145736 | tf_op jit(solution)/shard_map/ppermute | solution.py:134
  42.4 53.0 %collective-permute-start.5 = (bf16[4,4,32,1024]{3,2,1,0:T(8,128)(2,1)S(1)}, bf16[4,4,32,1024]{3,2,1,0:T(8,128)(2,1)}, u32[]{:S(2)}, u32[]{:S(2)}) collective-permute-start(bf16[4,4,32,1024]{3,2,1,0:T(8,128)(2,1)S(1)} %all-to-all-done.2.refs_0_), channel_id=1, source_target_pairs={{0,128},{64,192},{128,0},{192,64},{1,129},{65,193},{129,1},{193,65... | collective-permute-start | bytes 3145736 | tf_op jit(solution)/shard_map/ppermute | solution.py:134
  59.2 1.0 copy-start
  90.8 33.0 %all-to-all-start.1 = ((bf16[32,16,1024]{2,1,0:T(8,128)(2,1)}), bf16[32,16,1024]{2,1,0:T(8,128)(2,1)S(1)}, u32[]{:S(2)}, u32[]{:S(2)}) async-start(bf16[32,16,1024]{2,1,0:T(8,128)(2,1)} %bitcast.23), calls=%async_computation.1 | async-start | bytes 2097152 | tf_op jit(solution)/shard_map/all_to_all | solution.py:155
  94.7 31.7 %collective-permute-start = (bf16[4,4,32,1024]{3,2,1,0:T(8,128)(2,1)S(1)}, bf16[4,4,32,1024]{3,2,1,0:T(8,128)(2,1)}, u32[]{:S(2)}, u32[]{:S(2)}) collective-permute-start(bf16[4,4,32,1024]{3,2,1,0:T(8,128)(2,1)S(1)} %all-to-all-done.2.refs_0_), channel_id=1, source_target_pairs={{0,8},{8,0},{1,9},{9,1},{2,10},{10,2},{3,11},{11,3},{4,12},{12,4},... | collective-permute-start | bytes 3145736 | tf_op jit(solution)/shard_map/ppermute | solution.py:135
  94.9 30.4 %copy-start.2 = (bf16[4,4,32,1024]{3,2,1,0:T(8,128)(2,1)}, bf16[4,4,32,1024]{3,2,1,0:T(8,128)(2,1)S(1)}, u32[]{:S(2)}) copy-start(bf16[4,4,32,1024]{3,2,1,0:T(8,128)(2,1)S(1)} %collective-permute-done.1.refs_2_) | copy-start | bytes 3145732
  94.9 31.6 %collective-permute-start.2 = (bf16[4,4,32,1024]{3,2,1,0:T(8,128)(2,1)S(1)}, bf16[4,4,32,1024]{3,2,1,0:T(8,128)(2,1)}, u32[]{:S(2)}, u32[]{:S(2)}) collective-permute-start(bf16[4,4,32,1024]{3,2,1,0:T(8,128)(2,1)S(1)} %collective-permute-done.1.refs_2_), channel_id=1, source_target_pairs={{0,8},{8,0},{1,9},{9,1},{2,10},{10,2},{3,11},{11,3},{4,12},{12,4},... | collective-permute-start | bytes 3145736 | tf_op jit(solution)/shard_map/ppermute | solution.py:135
  95.3 31.1 %collective-permute-start.4 = (bf16[4,4,32,1024]{3,2,1,0:T(8,128)(2,1)}, bf16[4,4,32,1024]{3,2,1,0:T(8,128)(2,1)}, u32[]{:S(2)}, u32[]{:S(2)}) collective-permute-start(bf16[4,4,32,1024]{3,2,1,0:T(8,128)(2,1)} %collective-permute-done.3.refs_4_), channel_id=1, source_target_pairs={{0,8},{8,0},{1,9},{9,1},{2,10},{10,2},{3,11},{11,3},{4,12},{12,4},... | collective-permute-start | bytes 3145736 | tf_op jit(solution)/shard_map/ppermute | solution.py:135
  95.5 31.0 %collective-permute-start.6 = (bf16[4,4,32,1024]{3,2,1,0:T(8,128)(2,1)}, bf16[4,4,32,1024]{3,2,1,0:T(8,128)(2,1)}, u32[]{:S(2)}, u32[]{:S(2)}) collective-permute-start(bf16[4,4,32,1024]{3,2,1,0:T(8,128)(2,1)} %collective-permute-done.5.refs_6_), channel_id=1, source_target_pairs={{0,8},{8,0},{1,9},{9,1},{2,10},{10,2},{3,11},{11,3},{4,12},{12,4},... | collective-permute-start | bytes 3145736 | tf_op jit(solution)/shard_map/ppermute | solution.py:135
  133.8 17.0 %all-to-all-start.3 = ((bf16[32,32,128]{2,1,0:T(8,128)(2,1)}), bf16[32,32,128]{2,1,0:T(8,128)(2,1)S(1)}, u32[]{:S(2)}, u32[]{:S(2)}) async-start(bf16[32,32,128]{2,1,0:T(8,128)(2,1)} %bitcast.24), calls=%async_computation.3 | async-start | bytes 524288 | tf_op jit(solution)/shard_map/all_to_all | solution.py:166

commit v2 on v1

v2 whole, which is shorter than its diff:
```python
import functools

import jax
import jax.numpy as jnp
from jax import lax
from jax.experimental import pallas as pl
from jax.experimental.pallas import tpu as pltpu
from jax.sharding import Mesh, PartitionSpec as P

WIDE = ("y", "x", "core")
LANES = 128
BLK = 64
VMEM = pltpu.VMEM
SMEM = pltpu.SMEM
SHIFTS = (0, 1, 3, 2)


def vmem(n):
    return [pl.BlockSpec(memory_space=VMEM)] * n


def pair_halves(first, second):
    left = lax.broadcasted_iota(jnp.int32, first.shape, 1) < BLK
    low = jnp.where(left, first, pltpu.roll(second, BLK, 1))
    high = jnp.where(left, pltpu.roll(first, BLK, 1), second)
    return low, high


def spread_kernel(zero_code, c_hbm, go_hbm, gv_hbm, mask_hbm, out_ref, c_ref, ints, code, c_sem, int_sem):
    pairs, aux, width = c_ref.shape
    half = width // LANES
    loads = [pltpu.make_async_copy(c_hbm.at[j], c_ref.at[j], c_sem.at[j]) for j in range(pairs)]
    small = [pltpu.make_async_copy(ref, ints.at[i], int_sem.at[i]) for i, ref in enumerate((go_hbm, gv_hbm, mask_hbm))]
    for load in loads + small:
        load.start()
    for j in range(pairs):
        loads[j].wait()
        for g in range(aux // 16):
            x = c_ref[j, 16 * g : 16 * g + 16, :].astype(jnp.float32)
            x = pltpu.einshape("p(tl)->ptl", x, l=LANES)
            for i in range(4):
                d = 4 * g + i
                r = 2 * half * j
                for h in range(2):
                    one, two = x[4 * i + 2 * h], x[4 * i + 2 * h + 1]
                    low, high = pair_halves(one, two)
                    lanes = slice(LANES * h, LANES * h + LANES)
                    out_ref[d, r : r + half, lanes] = low.astype(jnp.bfloat16)
                    out_ref[d, r + half : r + 2 * half, lanes] = high.astype(jnp.bfloat16)
    rows = pairs * 2 * half
    number = ints.shape[2]
    for load in small:
        load.wait()
    code[...] = jnp.zeros_like(code)
    code[:pairs, :number] = ints[0].astype(jnp.float32)
    code[pairs : 2 * pairs, :number] = jnp.where(ints[2] != 0, ints[1], zero_code).astype(jnp.float32)
    for d in range(aux // 4):
        out_ref[d, rows : rows + 16, :] = code[...].astype(jnp.bfloat16)


def image_kernel(go_code, gv_code, w_ref, gt_ref, vb_ref, out_hbm, out_ref, sems):
    nsrc = w_ref.shape[0]
    pairs = out_ref.shape[1]
    number = nsrc * pairs
    step, batch = 4, 4

    @pl.loop(0, nsrc)
    def _(zd):
        for k0 in range(0, pairs, batch):
            ks = [zd * pairs + k0 + b for b in range(batch)]
            accs = [None] * batch
            for jb in range(0, number, step):
                lefts, rights = [[] for _ in ks], [[] for _ in ks]
                for j in range(jb, jb + step):
                    r = BLK * (j % pairs)
                    gt = [gt_ref[go_code[k, j]] for k in ks]
                    first = jnp.dot(
                        gt[0] if batch == 1 else jnp.concatenate(gt, axis=0),
                        w_ref[j // pairs, r : r + BLK, :],
                        preferred_element_type=jnp.float32,
                    ).astype(jnp.bfloat16)
                    for b, k in enumerate(ks):
                        own = first[BLK * b : BLK * b + BLK]
                        lefts[b].append(jnp.concatenate([own[:, :LANES], own[:, LANES:]], axis=0))
                        rights[b].append(vb_ref[gv_code[k, j]])
                for b in range(batch):
                    part = jnp.dot(
                        jnp.concatenate(lefts[b], axis=1),
                        jnp.concatenate(rights[b], axis=0),
                        preferred_element_type=jnp.float32,
                    )
                    accs[b] = part if accs[b] is None else accs[b] + part
            for b, acc in enumerate(accs):
                tiles = []
                for h in range(2):
                    tiles += pair_halves(acc[BLK * h : BLK * h + 32], acc[BLK * h + 32 : BLK * h + 64])
                out_ref[zd, k0 + b] = pltpu.einshape("ptl->p(tl)", jnp.stack(tiles)).astype(jnp.bfloat16)
        pltpu.make_async_copy(out_ref.at[zd], out_hbm.at[:, zd], sems.at[zd]).start()

    for zd in range(nsrc):
        pltpu.make_async_copy(out_ref.at[zd], out_hbm.at[:, zd], sems.at[zd]).wait()


def chi_kernel(scale, pos, im_ref, *refs):
    pieces, out_ref = refs[:8], refs[8]
    lower = lax.rem(lax.broadcasted_iota(jnp.int32, (32, LANES), 1), 64) < 32
    swapped = jnp.full((32, LANES), pos[2], jnp.int32) != 0
    for s in range(4):
        order = [lax.rem(pos[0] + 4 - x, 4) for x in range(4)]
        rhs = jnp.concatenate([pieces[2 * s + c][order[x]] for x in range(4) for c in range(2)], axis=0)
        acc = lax.dot_general(
            im_ref[...], rhs, (((1,), (1,)), ((), ())), preferred_element_type=jnp.float32
        )
        acc = acc * scale
        y = lax.rem(pos[1] + 4 - SHIFTS[s], 4)
        for xd in range(4):
            for h in range(2):
                tile = acc[32 * xd : 32 * xd + 32, LANES * h : LANES * h + LANES]
                turned = jnp.where(lower, pltpu.roll(tile, 96, 1), pltpu.roll(tile, 32, 1))
                out_ref[xd, 2 * y + h] = jnp.where(swapped, turned, tile).astype(jnp.bfloat16)


def local(three_centre, go_blocks, gv_blocks, go_index, gv_index, source_mask):
    pairs, aux, width = three_centre.shape
    nz = lax.axis_size("z")
    nx = lax.axis_size("x")
    number = pairs * nz
    blocks = go_blocks.shape[0]
    scale = float((number * width) ** -0.5)

    rows = pairs * BLK
    spread = pl.pallas_call(
        functools.partial(spread_kernel, blocks),
        out_shape=jax.ShapeDtypeStruct((nz, rows + 16, 4 * BLK), jnp.bfloat16),
        in_specs=[pl.BlockSpec(memory_space=pl.ANY)] * 4,
        out_specs=vmem(1)[0],
        scratch_shapes=[
            VMEM((pairs, aux, width), jnp.bfloat16),
            VMEM((3,) + go_index.shape, jnp.int32),
            VMEM((16, 4 * BLK), jnp.float32),
            pltpu.SemaphoreType.DMA((pairs,)),
            pltpu.SemaphoreType.DMA((3,)),
        ],
        name="spread",
    )(three_centre, go_index, gv_index, source_mask)
    w = lax.all_to_all(spread, "z", 0, 0, tiled=True)

    x = lax.axis_index("x")
    cx = []
    for s in range(nx):
        piece = lax.dynamic_index_in_dim(three_centre, lax.rem(x + s, nx), 0, keepdims=False)
        cx.append(piece if s == 0 else lax.ppermute(piece, "x", [(i, (i + s) % nx) for i in range(nx)]))
    cx = jnp.stack(cx)
    pieces = []
    for s in SHIFTS:
        own = cx if s == 0 else lax.ppermute(cx, "y", [(i, (i + s) % 4) for i in range(4)])
        pieces += [own, lax.ppermute(own, "core", [(0, 1), (1, 0)])]

    gt = go_blocks.reshape(blocks, 32, 2, 32, 2).transpose(0, 4, 3, 2, 1).reshape(blocks, BLK, BLK)
    zero = jnp.zeros_like(gv_blocks)
    vb = jnp.concatenate(
        [jnp.concatenate([gv_blocks, zero], axis=2), jnp.concatenate([zero, gv_blocks], axis=2)], axis=1
    )
    vb = jnp.concatenate([vb, jnp.zeros((1, LANES, LANES), jnp.bfloat16)], axis=0)

    got = w[:, rows : rows + 2 * pairs, :number].astype(jnp.int32)
    go_code = got[:, :pairs].reshape(number, number)
    gv_code = got[:, pairs:].reshape(number, number)
    image = pl.pallas_call(
        image_kernel,
        out_shape=jax.ShapeDtypeStruct((nx, nz, 4, width), jnp.bfloat16),
        in_specs=[pl.BlockSpec(memory_space=SMEM)] * 2 + vmem(3),
        out_specs=pl.BlockSpec(memory_space=pl.ANY),
        scratch_shapes=[VMEM((nz, nx, 4, width), jnp.bfloat16), pltpu.SemaphoreType.DMA((nz,))],
        compiler_params=pltpu.CompilerParams(vmem_limit_bytes=24 << 20),
        name="image",
    )(go_code, gv_code, w, gt, vb)
    image = lax.all_to_all(image.reshape(nx * nz, 4, width), ("x", "z"), 0, 0, tiled=True)

    part = pl.pallas_call(
        functools.partial(chi_kernel, scale),
        out_shape=jax.ShapeDtypeStruct((nx, nz, aux, 4 * aux), jnp.bfloat16),
        in_specs=[pl.BlockSpec(memory_space=SMEM)] + vmem(9),
        out_specs=vmem(1)[0],
        compiler_params=pltpu.CompilerParams(vmem_limit_bytes=24 << 20),
        name="chi",
    )(jnp.stack([x, lax.axis_index("y"), lax.axis_index("core")]), image.reshape(nx * nz * 4, width), *pieces)
    part = lax.all_to_all(part.reshape(nx * nz, aux, 4 * aux), ("x", "z"), 0, 0, tiled=True)
    return jnp.sum(part.astype(jnp.float32), axis=0)


def solution(mesh):
    grid = Mesh(mesh.devices.reshape(4, 4, 2, 8), WIDE + ("z",))
    rows = P("z", None)
    return jax.shard_map(
        local,
        mesh=grid,
        in_specs=(P("z", WIDE, None), P(), P(), rows, rows, rows),
        out_specs=P(WIDE, "z"),
        check_vma=False,
    )
```

time: 152 us -> 126 us (0.83)
  waiting for transfers between devices: 66.4 us -> 41 us
  blocking collectives: 0 us -> 16.7 us
  Pallas kernels: 41 us -> 32.6 us
  local copies, waits for them, and re-layouts: 15.5 us -> 9.99 us
  starting transfers between devices: 26.4 us -> 22 us
    all_to_all x3 -> x1, waiting for transfers between devices: 51.2 us -> 20.7 us  [local(): lax.all_to_all(image.reshape(nx * nz, 4, width), ('x', 'z'), 0, 0, tiled=...]
    all_to_all x0 -> x1, blocking collectives: none -> 16.7 us  [local(): lax.all_to_all(part.reshape(nx * nz, aux, 4 * aux), ('x', 'z'), 0, 0, til...]
    all_to_all x1, waiting for transfers between devices: 15.2 us -> 5.76 us  [local(): w = lax.all_to_all(spread, 'z', 0, 0, tiled=True)]
    all_to_all x3 -> x1, starting transfers between devices: 13.3 us -> 4.82 us  [local(): lax.all_to_all(image.reshape(nx * nz, 4, width), ('x', 'z'), 0, 0, tiled=...]
    ppermute x3, waiting for transfers between devices: 0.01 us -> 7.39 us  [local(): lax.ppermute(cx, 'y', [(i, (i + s) % 4) for i in range(4)])]
    ppermute x4 -> x7, waiting for transfers between devices: 0.01 us -> 7.14 us  [the longest x3 7.13 us: local(): lax.ppermute(piece, 'x', [(i, (i + s) % nx) for i in range(nx)])]
    pallas_call x2, Pallas kernels: 33.7 us -> 26.8 us  [the longest x1 23.9 us: local(): pl.pallas_call(image_kernel, out_shape=jax.ShapeDtypeStruct((nx, nz, 4, w...]
    ppermute x4 -> x7, starting transfers between devices: 1.09 us -> 5.14 us  [the longest x3 4.44 us: local(): lax.ppermute(piece, 'x', [(i, (i + s) % nx) for i in range(nx)])]
  transfers between devices with their start and end apart: 11 -> 12, of which waited for: 4 -> 5; matrix products, arithmetic and copies ran while one was open for 9% -> 8% of each run, Pallas kernels for 22% -> 19%
where the time goes in v2:
time: 126 us
  waiting for transfers between devices  41 us (33%)
  Pallas kernels  32.6 us (26%)
  starting transfers between devices  22 us (17%)
  blocking collectives  16.7 us (13%)
  local copies, waits for them, and re-layouts  9.99 us (8%)
  other arithmetic  3.58 us (3%)
    pallas_call x1, Pallas kernels, local(): pl.pallas_call(image_kernel, out_shape=jax.ShapeDtypeStruct((nx, nz, 4, w...  23.9 us
    all_to_all x1, waiting for transfers between devices, local(): lax.all_to_all(image.reshape(nx * nz, 4, width), ('x', 'z'), 0, 0, tiled=...  20.7 us
    all_to_all x1, blocking collectives, local(): lax.all_to_all(part.reshape(nx * nz, aux, 4 * aux), ('x', 'z'), 0, 0, til...  16.7 us
    all_to_all x1, starting transfers between devices, local(): w = lax.all_to_all(spread, 'z', 0, 0, tiled=True)  8.48 us
    ppermute x3, waiting for transfers between devices, local(): lax.ppermute(cx, 'y', [(i, (i + s) % 4) for i in range(4)])  7.39 us
    ppermute x3, waiting for transfers between devices, local(): lax.ppermute(piece, 'x', [(i, (i + s) % nx) for i in range(nx)])  7.13 us
    pallas_call x1, Pallas kernels, local(): pl.pallas_call(functools.partial(chi_kernel, scale), out_shape=jax.ShapeD...  5.8 us
    all_to_all x1, waiting for transfers between devices, local(): w = lax.all_to_all(spread, 'z', 0, 0, tiled=True)  5.76 us
  transfers between devices with their start and end apart: 12, of which 5 were waited for; matrix products, arithmetic and copies ran while one was open for 8% of the time, Pallas kernels for 19%

profile of v2, /device:TPU:16, one launch (start us, length us, event | category | flops | bytes accessed | tf_op | source)
XLA Modules:
  0.0 126.0 jit_solution(1894605396156976548)
XLA Ops:
  0.0 2.9 %spread.1 = bf16[8,272,256]{2,1,0:T(8,128)(2,1)} custom-call(bf16[4,32,4096]{2,1,0:T(8,128)(2,1)} %c_hbm.1, s32[4,32]{1,0:T(4,128)} %go_hbm.1, s32[4,32]{1,0:T(4,128)} %gv_hbm.1, s32[4,32]{1,0:T(4,128)} %mask_hbm.1), custom_call_target="tpu_custom_call" | custom-call | tf_op jit(solution)/shard_map/spread/pallas_call | solution.py:132
  2.9 8.5 %all-to-all-start = ((bf16[8,272,256]{2,1,0:T(8,128)(2,1)}), bf16[8,272,256]{2,1,0:T(8,128)(2,1)S(1)}, u32[]{:S(2)}, u32[]{:S(2)}) async-start(bf16[8,272,256]{2,1,0:T(8,128)(2,1)} %spread.1), calls=%async_computation | async-start | bytes 2228224 | tf_op jit(solution)/shard_map/all_to_all | solution.py:146
  11.4 0.9 constant_dynamic-slice_fusion
  12.3 2.8 %collective-permute-start.2 = (bf16[32,4096]{1,0:T(8,128)(2,1)}, bf16[32,4096]{1,0:T(8,128)(2,1)}, u32[]{:S(2)}, u32[]{:S(2)}) collective-permute-start(bf16[32,4096]{1,0:T(8,128)(2,1)} %get-tuple-element.7), channel_id=1, source_target_pairs={{0,48},{16,0},{32,16},{48,32},{1,49},{17,1},{33,17},{49,33},{2,50}... | collective-permute-start | bytes 786440 | tf_op jit(solution)/shard_map/ppermute | solution.py:152
  15.1 0.8 collective-permute-start.1
  15.9 0.9 collective-permute-start
  16.8 2.2 %copy.8 = bf16[64,64,64]{0,2,1:T(8,128)(2,1)S(1)} copy(bf16[64,64,64]{2,1,0:T(8,128)(2,1)} %param.7) | data formatting | bytes 1048576 | tf_op args[1]
  19.7 2.4 %copy.10.gt_ref = bf16[64,64,64]{2,1,0:T(8,128)(2,1)} copy(bf16[64,64,64]{0,2,1:T(8,128)(2,1)S(1)} %bitcast.24) | data formatting | bytes 1048576 | tf_op jit(solution)/shard_map/reshape | solution.py:159
  22.9 3.5 %collective-permute-done.2 = bf16[32,4096]{1,0:T(8,128)(2,1)} collective-permute-done((bf16[32,4096]{1,0:T(8,128)(2,1)}, bf16[32,4096]{1,0:T(8,128)(2,1)}, u32[]{:S(2)}, u32[]{:S(2)}) %collective-permute-start.2) | collective-permute-done | bytes 262176 | tf_op jit(solution)/shard_map/ppermute | solution.py:152
  26.3 3.7 %collective-permute-done = bf16[32,4096]{1,0:T(8,128)(2,1)} collective-permute-done((bf16[32,4096]{1,0:T(8,128)(2,1)}, bf16[32,4096]{1,0:T(8,128)(2,1)}, u32[]{:S(2)}, u32[]{:S(2)}) %collective-permute-start) | collective-permute-done | bytes 262176 | tf_op jit(solution)/shard_map/ppermute | solution.py:152
  30.0 2.2 %pad_maximum_fusion.refs_0_ = bf16[4,32,4096]{2,1,0:T(8,128)(2,1)} fusion(bf16[1,32,4096]{2,1,0:T(8,128)(2,1)} %bitcast.14, bf16[1,32,4096]{2,1,0:T(8,128)(2,1)} %bitcast.12, bf16[1,32,4096]{2,1,0:T(8,128)(2,1)} %bitcast.10, bf16[1,32,4096]{2,1,0:T(8,128)(2,1)S(1)} %get-tuple-element.5), kind=kLoop, calls=%fused_computation.5 | loop fusion | flops 1572864 | bytes 2097152 | tf_op jit(solution)/shard_map/stack | solution.py:153
  32.2 1.3 %collective-permute-start.4 = (bf16[4,32,4096]{2,1,0:T(8,128)(2,1)}, bf16[4,32,4096]{2,1,0:T(8,128)(2,1)}, u32[]{:S(2)}, u32[]{:S(2)}) collective-permute-start(bf16[4,32,4096]{2,1,0:T(8,128)(2,1)} %pad_maximum_fusion.refs_0_), channel_id=1, source_target_pairs={{0,64},{64,128},{128,192},{192,0},{1,65},{65,129},{129,193},{193,1... | collective-permute-start | bytes 3145736 | tf_op jit(solution)/shard_map/ppermute | solution.py:156
  33.5 0.7 collective-permute-start.6
  34.2 1.5 %collective-permute-start.8 = (bf16[4,32,4096]{2,1,0:T(8,128)(2,1)}, bf16[4,32,4096]{2,1,0:T(8,128)(2,1)}, u32[]{:S(2)}, u32[]{:S(2)}) collective-permute-start(bf16[4,32,4096]{2,1,0:T(8,128)(2,1)} %pad_maximum_fusion.refs_0_), channel_id=1, source_target_pairs={{0,128},{64,192},{128,0},{192,64},{1,129},{65,193},{129,1},{193,65... | collective-permute-start | bytes 3145736 | tf_op jit(solution)/shard_map/ppermute | solution.py:156
  35.8 5.8 %all-to-all-done.w_ref = bf16[8,272,256]{2,1,0:T(8,128)(2,1)S(1)} async-done(((bf16[8,272,256]{2,1,0:T(8,128)(2,1)}), bf16[8,272,256]{2,1,0:T(8,128)(2,1)S(1)}, u32[]{:S(2)}, u32[]{:S(2)}) %all-to-all-start) | async-done | bytes 1114144 | tf_op jit(solution)/shard_map/all_to_all | solution.py:146
  41.6 1.2 copy-done.1
  42.8 23.9 %image.1 = bf16[4,8,4,4096]{3,2,1,0:T(4,128)(2,1)S(1)} custom-call(s32[32,32]{1,0:T(8,128)S(1)} %bitcast.23, s32[32,32]{1,0:T(8,128)S(1)} %bitcast.22, bf16[8,272,256]{2,1,0:T(8,128)(2,1)S(1)} %all-to-all-done.w_ref, bf16[64,64,64]{2,1,0:T(8,128)(2,1)S(1)} %copy-done.1, bf16[65,128,128]{2,1,0:T(8,128)(2,1)S(1)} %concatenate.15.vb_ref), custom_call_target="tpu_custom_call" | custom-call | tf_op jit(solution)/shard_map/image/pallas_call | solution.py:169
  66.7 1.0 copy-done
  67.8 4.8 %all-to-all-start.1 = ((bf16[32,4,4096]{2,1,0:T(4,128)(2,1)}), bf16[32,4,4096]{2,1,0:T(4,128)(2,1)}, u32[]{:S(2)}, u32[]{:S(2)}) async-start(bf16[32,4,4096]{2,1,0:T(4,128)(2,1)} %bitcast.20), calls=%async_computation.1 | async-start | bytes 2097152 | tf_op jit(solution)/shard_map/all_to_all | solution.py:178
  72.7 7.4 %collective-permute-done.4.refs_2_ = bf16[4,32,4096]{2,1,0:T(8,128)(2,1)} collective-permute-done((bf16[4,32,4096]{2,1,0:T(8,128)(2,1)}, bf16[4,32,4096]{2,1,0:T(8,128)(2,1)}, u32[]{:S(2)}, u32[]{:S(2)}) %collective-permute-start.4) | collective-permute-done | bytes 1048608 | tf_op jit(solution)/shard_map/ppermute | solution.py:156
  80.8 20.7 %all-to-all-done.1 = bf16[32,4,4096]{2,1,0:T(4,128)(2,1)} async-done(((bf16[32,4,4096]{2,1,0:T(4,128)(2,1)}), bf16[32,4,4096]{2,1,0:T(4,128)(2,1)}, u32[]{:S(2)}, u32[]{:S(2)}) %all-to-all-start.1) | async-done | bytes 1048608 | tf_op jit(solution)/shard_map/all_to_all | solution.py:178
  101.5 1.3 %reshape.26.im_ref = bf16[128,4096]{1,0:T(8,128)(2,1)S(1)} reshape(bf16[32,4,4096]{2,1,0:T(4,128)(2,1)} %all-to-all-done.1) | data formatting | bytes 2097152 | tf_op jit(solution)/shard_map/reshape | solution.py:187
  102.9 5.8 %chi.1 = bf16[4,8,32,128]{3,2,1,0:T(8,128)(2,1)S(1)} custom-call(s32[3]{0:T(128)S(1)} %pad_add_fusion.pos, bf16[128,4096]{1,0:T(8,128)(2,1)S(1)} %reshape.26.im_ref, bf16[4,32,4096]{2,1,0:T(8,128)(2,1)} %pad_maximum_fusion.refs_0_, bf16[4,32,4096]{2,1,0:T(8,128)(2,1)S(1)} %collective-permute-done.3.refs_1_, ...), custom_call_target="tpu_custom_call" | custom-call | tf_op jit(solution)/shard_map/chi/pallas_call | solution.py:180
  108.7 16.7 %all_to_all.15 = bf16[32,32,128]{2,1,0:T(8,128)(2,1)S(1)} all-to-all(bf16[32,32,128]{2,1,0:T(8,128)(2,1)S(1)} %bitcast.21), channel_id=1, replica_groups=mesh['y'=4,'x'=4,'core'=2,'z'=8] {'x','z'}, dimensions={0} | all-to-all | bytes 524288 | tf_op jit(solution)/shard_map/all_to_all | solution.py:188
  (24 shorter events, 2.9 us)
Async XLA Ops:
  0.0 11.4 %copy-start.2 = (bf16[4,32,4096]{2,1,0:T(8,128)(2,1)S(1)}, bf16[4,32,4096]{2,1,0:T(8,128)(2,1)}, u32[]{:S(2)}) copy-start(bf16[4,32,4096]{2,1,0:T(8,128)(2,1)} %c_hbm.1) | copy-start | bytes 3145732
  2.9 38.7 %all-to-all-start = ((bf16[8,272,256]{2,1,0:T(8,128)(2,1)}), bf16[8,272,256]{2,1,0:T(8,128)(2,1)S(1)}, u32[]{:S(2)}, u32[]{:S(2)}) async-start(bf16[8,272,256]{2,1,0:T(8,128)(2,1)} %spread.1), calls=%async_computation | async-start | bytes 2228224 | tf_op jit(solution)/shard_map/all_to_all | solution.py:146
  12.3 14.0 %collective-permute-start.2 = (bf16[32,4096]{1,0:T(8,128)(2,1)}, bf16[32,4096]{1,0:T(8,128)(2,1)}, u32[]{:S(2)}, u32[]{:S(2)}) collective-permute-start(bf16[32,4096]{1,0:T(8,128)(2,1)} %get-tuple-element.7), channel_id=1, source_target_pairs={{0,48},{16,0},{32,16},{48,32},{1,49},{17,1},{33,17},{49,33},{2,50}... | collective-permute-start | bytes 786440 | tf_op jit(solution)/shard_map/ppermute | solution.py:152
  15.1 11.3 %collective-permute-start.1 = (bf16[32,4096]{1,0:T(8,128)(2,1)}, bf16[32,4096]{1,0:T(8,128)(2,1)}, u32[]{:S(2)}, u32[]{:S(2)}) collective-permute-start(bf16[32,4096]{1,0:T(8,128)(2,1)} %get-tuple-element.8), channel_id=1, source_target_pairs={{0,32},{16,48},{32,0},{48,16},{1,33},{17,49},{33,1},{49,17},{2,34}... | collective-permute-start | bytes 786440 | tf_op jit(solution)/shard_map/ppermute | solution.py:152
  15.9 14.1 %collective-permute-start = (bf16[32,4096]{1,0:T(8,128)(2,1)}, bf16[32,4096]{1,0:T(8,128)(2,1)}, u32[]{:S(2)}, u32[]{:S(2)}) collective-permute-start(bf16[32,4096]{1,0:T(8,128)(2,1)} %get-tuple-element.6), channel_id=1, source_target_pairs={{0,16},{16,32},{32,48},{48,0},{1,17},{17,33},{33,49},{49,1},{2,18}... | collective-permute-start | bytes 786440 | tf_op jit(solution)/shard_map/ppermute | solution.py:152
  19.7 2.4 %copy-start.3 = (bf16[64,64,64]{2,1,0:T(8,128)(2,1)S(1)}, bf16[64,64,64]{2,1,0:T(8,128)(2,1)}, u32[]{:S(2)}) copy-start(bf16[64,64,64]{2,1,0:T(8,128)(2,1)} %param.8) | copy-start | bytes 1572868
  32.2 47.9 %collective-permute-start.4 = (bf16[4,32,4096]{2,1,0:T(8,128)(2,1)}, bf16[4,32,4096]{2,1,0:T(8,128)(2,1)}, u32[]{:S(2)}, u32[]{:S(2)}) collective-permute-start(bf16[4,32,4096]{2,1,0:T(8,128)(2,1)} %pad_maximum_fusion.refs_0_), channel_id=1, source_target_pairs={{0,64},{64,128},{128,192},{192,0},{1,65},{65,129},{129,193},{193,1... | collective-permute-start | bytes 3145736 | tf_op jit(solution)/shard_map/ppermute | solution.py:156
  33.5 46.6 %collective-permute-start.6 = (bf16[4,32,4096]{2,1,0:T(8,128)(2,1)}, bf16[4,32,4096]{2,1,0:T(8,128)(2,1)}, u32[]{:S(2)}, u32[]{:S(2)}) collective-permute-start(bf16[4,32,4096]{2,1,0:T(8,128)(2,1)} %pad_maximum_fusion.refs_0_), channel_id=1, source_target_pairs={{0,192},{64,0},{128,64},{192,128},{1,193},{65,1},{129,65},{193,129... | collective-permute-start | bytes 3145736 | tf_op jit(solution)/shard_map/ppermute | solution.py:156
  34.2 46.4 %collective-permute-start.8 = (bf16[4,32,4096]{2,1,0:T(8,128)(2,1)}, bf16[4,32,4096]{2,1,0:T(8,128)(2,1)}, u32[]{:S(2)}, u32[]{:S(2)}) collective-permute-start(bf16[4,32,4096]{2,1,0:T(8,128)(2,1)} %pad_maximum_fusion.refs_0_), channel_id=1, source_target_pairs={{0,128},{64,192},{128,0},{192,64},{1,129},{65,193},{129,1},{193,65... | collective-permute-start | bytes 3145736 | tf_op jit(solution)/shard_map/ppermute | solution.py:156
  41.6 1.2 copy-start.1
  66.7 1.1 copy-start
  67.8 33.7 %all-to-all-start.1 = ((bf16[32,4,4096]{2,1,0:T(4,128)(2,1)}), bf16[32,4,4096]{2,1,0:T(4,128)(2,1)}, u32[]{:S(2)}, u32[]{:S(2)}) async-start(bf16[32,4,4096]{2,1,0:T(4,128)(2,1)} %bitcast.20), calls=%async_computation.1 | async-start | bytes 2097152 | tf_op jit(solution)/shard_map/all_to_all | solution.py:178
  72.6 30.2 %collective-permute-start.3 = (bf16[4,32,4096]{2,1,0:T(8,128)(2,1)}, bf16[4,32,4096]{2,1,0:T(8,128)(2,1)S(1)}, u32[]{:S(2)}, u32[]{:S(2)}) collective-permute-start(bf16[4,32,4096]{2,1,0:T(8,128)(2,1)} %pad_maximum_fusion.refs_0_), channel_id=1, source_target_pairs={{0,8},{8,0},{1,9},{9,1},{2,10},{10,2},{3,11},{11,3},{4,12},{12,4},... | collective-permute-start | bytes 3145736 | tf_op jit(solution)/shard_map/ppermute | solution.py:157
  80.1 22.8 %collective-permute-start.5 = (bf16[4,32,4096]{2,1,0:T(8,128)(2,1)}, bf16[4,32,4096]{2,1,0:T(8,128)(2,1)S(1)}, u32[]{:S(2)}, u32[]{:S(2)}) collective-permute-start(bf16[4,32,4096]{2,1,0:T(8,128)(2,1)} %collective-permute-done.4.refs_2_), channel_id=1, source_target_pairs={{0,8},{8,0},{1,9},{9,1},{2,10},{10,2},{3,11},{11,3},{4,12},{12,4},... | collective-permute-start | bytes 3145736 | tf_op jit(solution)/shard_map/ppermute | solution.py:157
  80.1 22.8 %collective-permute-start.7 = (bf16[4,32,4096]{2,1,0:T(8,128)(2,1)}, bf16[4,32,4096]{2,1,0:T(8,128)(2,1)}, u32[]{:S(2)}, u32[]{:S(2)}) collective-permute-start(bf16[4,32,4096]{2,1,0:T(8,128)(2,1)} %collective-permute-done.6.refs_4_), channel_id=1, source_target_pairs={{0,8},{8,0},{1,9},{9,1},{2,10},{10,2},{3,11},{11,3},{4,12},{12,4},... | collective-permute-start | bytes 3145736 | tf_op jit(solution)/shard_map/ppermute | solution.py:157
  80.6 22.3 %collective-permute-start.9 = (bf16[4,32,4096]{2,1,0:T(8,128)(2,1)}, bf16[4,32,4096]{2,1,0:T(8,128)(2,1)}, u32[]{:S(2)}, u32[]{:S(2)}) collective-permute-start(bf16[4,32,4096]{2,1,0:T(8,128)(2,1)} %collective-permute-done.8.refs_6_), channel_id=1, source_target_pairs={{0,8},{8,0},{1,9},{9,1},{2,10},{10,2},{3,11},{11,3},{4,12},{12,4},... | collective-permute-start | bytes 3145736 | tf_op jit(solution)/shard_map/ppermute | solution.py:157

commit v3 on v2

--- a/solution.py
+++ b/solution.py
@@ -58,14 +58,24 @@
         out_ref[d, rows : rows + 16, :] = code[...].astype(jnp.bfloat16)
 
 
-def image_kernel(go_code, gv_code, w_ref, gt_ref, vb_ref, out_hbm, out_ref, sems):
+def image_kernel(go_code, gv_code, w_ref, gt_ref, vb_ref, out_hbm, out_ref, stage, sems):
     nsrc = w_ref.shape[0]
     pairs = out_ref.shape[1]
     number = nsrc * pairs
-    step, batch = 4, 4
+    step, batch = 16, 4
+
+    def finish(zd):
+        for kk in range(pairs):
+            out_ref[zd, kk] = pltpu.einshape("ptl->p(tl)", stage[kk]).astype(jnp.bfloat16)
+
+    def send(zd):
+        return pltpu.make_async_copy(out_ref.at[zd], out_hbm.at[:, zd], sems.at[zd])
+
+    stage[...] = jnp.zeros_like(stage)
 
     @pl.loop(0, nsrc)
     def _(zd):
+        finish(lax.max(zd - 1, 0))
         for k0 in range(0, pairs, batch):
             ks = [zd * pairs + k0 + b for b in range(batch)]
             accs = [None] * batch
@@ -91,26 +101,31 @@
                     )
                     accs[b] = part if accs[b] is None else accs[b] + part
             for b, acc in enumerate(accs):
-                tiles = []
                 for h in range(2):
-                    tiles += pair_halves(acc[BLK * h : BLK * h + 32], acc[BLK * h + 32 : BLK * h + 64])
-                out_ref[zd, k0 + b] = pltpu.einshape("ptl->p(tl)", jnp.stack(tiles)).astype(jnp.bfloat16)
-        pltpu.make_async_copy(out_ref.at[zd], out_hbm.at[:, zd], sems.at[zd]).start()
-
+                    tiles = pair_halves(acc[BLK * h : BLK * h + 32], acc[BLK * h + 32 : BLK * h + 64])
+                    stage[k0 + b, 2 * h], stage[k0 + b, 2 * h + 1] = tiles
+
+        @pl.when(zd > 0)
+        def _():
+            send(zd - 1).start()
+
+    finish(nsrc - 1)
+    send(nsrc - 1).start()
     for zd in range(nsrc):
-        pltpu.make_async_copy(out_ref.at[zd], out_hbm.at[:, zd], sems.at[zd]).wait()
+        send(zd).wait()
 
 
 def chi_kernel(scale, pos, im_ref, *refs):
-    pieces, out_ref = refs[:8], refs[8]
+    pieces, out_ref, rows = refs[:8], refs[8], refs[9]
     lower = lax.rem(lax.broadcasted_iota(jnp.int32, (32, LANES), 1), 64) < 32
     swapped = jnp.full((32, LANES), pos[2], jnp.int32) != 0
+    for i in range(0, im_ref.shape[0], 4):
+        four = [im_ref[i + b].astype(jnp.float32) for b in range(4)]
+        rows[4 * i : 4 * i + 16, :] = jnp.concatenate(four, axis=0).astype(jnp.bfloat16)
+    order = [lax.rem(pos[0] + 4 - x, 4) for x in range(4)]
     for s in range(4):
-        order = [lax.rem(pos[0] + 4 - x, 4) for x in range(4)]
         rhs = jnp.concatenate([pieces[2 * s + c][order[x]] for x in range(4) for c in range(2)], axis=0)
-        acc = lax.dot_general(
-            im_ref[...], rhs, (((1,), (1,)), ((), ())), preferred_element_type=jnp.float32
-        )
+        acc = lax.dot_general(rows[...], rhs, (((1,), (1,)), ((), ())), preferred_element_type=jnp.float32)
         acc = acc * scale
         y = lax.rem(pos[1] + 4 - SHIFTS[s], 4)
         for xd in range(4):
@@ -170,8 +185,12 @@
         image_kernel,
         out_shape=jax.ShapeDtypeStruct((nx, nz, 4, width), jnp.bfloat16),
         in_specs=[pl.BlockSpec(memory_space=SMEM)] * 2 + vmem(3),
-        out_specs=pl.BlockSpec(memory_space=pl.ANY),
-        scratch_shapes=[VMEM((nz, nx, 4, width), jnp.bfloat16), pltpu.SemaphoreType.DMA((nz,))],
+        out_specs=pl.BlockSpec(memory_space=pltpu.HBM),
+        scratch_shapes=[
+            VMEM((nz, nx, 4, width), jnp.bfloat16),
+            VMEM((pairs, 4, width // LANES, LANES), jnp.float32),
+            pltpu.SemaphoreType.DMA((nz,)),
+        ],
         compiler_params=pltpu.CompilerParams(vmem_limit_bytes=24 << 20),
         name="image",
     )(go_code, gv_code, w, gt, vb)
@@ -182,9 +201,10 @@
         out_shape=jax.ShapeDtypeStruct((nx, nz, aux, 4 * aux), jnp.bfloat16),
         in_specs=[pl.BlockSpec(memory_space=SMEM)] + vmem(9),
         out_specs=vmem(1)[0],
+        scratch_shapes=[VMEM((nx * nz * 4, width), jnp.bfloat16)],
         compiler_params=pltpu.CompilerParams(vmem_limit_bytes=24 << 20),
         name="chi",
-    )(jnp.stack([x, lax.axis_index("y"), lax.axis_index("core")]), image.reshape(nx * nz * 4, width), *pieces)
+    )(jnp.stack([x, lax.axis_index("y"), lax.axis_index("core")]), image, *pieces)
     part = lax.all_to_all(part.reshape(nx * nz, aux, 4 * aux), ("x", "z"), 0, 0, tiled=True)
     return jnp.sum(part.astype(jnp.float32), axis=0)
 

time: 126 us -> 122 us (0.968)
  Pallas kernels: 32.6 us -> 29.5 us
  local copies, waits for them, and re-layouts: 9.99 us -> 8.58 us
    all_to_all x1, waiting for transfers between devices: 20.7 us -> 12 us  [local(): lax.all_to_all(image.reshape(nx * nz, 4, width), ('x', 'z'), 0, 0, tiled=...]
    ppermute x4, waiting for transfers between devices: 0.01 us -> 5.31 us  [local(): pieces += [own, lax.ppermute(own, 'core', [(0, 1), (1, 0)])]]
    ppermute x3, waiting for transfers between devices: 7.39 us -> 10.7 us  [local(): lax.ppermute(cx, 'y', [(i, (i + s) % 4) for i in range(4)])]
    pallas_call x1, Pallas kernels: 23.9 us -> 20.8 us  [local(): pl.pallas_call(image_kernel, out_shape=jax.ShapeDtypeStruct((nx, nz, 4, w...]
    reshape x1 -> x0, local copies, waits for them, and re-layouts: 1.34 us -> none  [local(): image.reshape(nx * nz * 4, width)]
  transfers between devices with their start and end apart: 12 -> 12, of which waited for: 5 -> 8; matrix products, arithmetic and copies ran while one was open for 8% -> 8% of each run, Pallas kernels for 19% -> 17%
where the time goes in v3:
time: 122 us; the launch traced here: 121 us
  waiting for transfers between devices  40.9 us (34%)
  Pallas kernels  29.5 us (24%)
  starting transfers between devices  21.9 us (18%)
  blocking collectives  16.7 us (14%)
  local copies, waits for them, and re-layouts  8.58 us (7%)
  other arithmetic  3.58 us (3%)
    pallas_call x1, Pallas kernels, local(): pl.pallas_call(image_kernel, out_shape=jax.ShapeDtypeStruct((nx, nz, 4, w...  20.8 us
    all_to_all x1, blocking collectives, local(): lax.all_to_all(part.reshape(nx * nz, aux, 4 * aux), ('x', 'z'), 0, 0, til...  16.7 us
    all_to_all x1, waiting for transfers between devices, local(): lax.all_to_all(image.reshape(nx * nz, 4, width), ('x', 'z'), 0, 0, tiled=...  12 us
    ppermute x3, waiting for transfers between devices, local(): lax.ppermute(cx, 'y', [(i, (i + s) % 4) for i in range(4)])  10.7 us
    all_to_all x1, starting transfers between devices, local(): w = lax.all_to_all(spread, 'z', 0, 0, tiled=True)  8.48 us
    ppermute x3, waiting for transfers between devices, local(): lax.ppermute(piece, 'x', [(i, (i + s) % nx) for i in range(nx)])  7.13 us
    pallas_call x1, Pallas kernels, local(): pl.pallas_call(functools.partial(chi_kernel, scale), out_shape=jax.ShapeD...  5.8 us
    all_to_all x1, waiting for transfers between devices, local(): w = lax.all_to_all(spread, 'z', 0, 0, tiled=True)  5.76 us
  transfers between devices with their start and end apart: 12, of which 8 were waited for; matrix products, arithmetic and copies ran while one was open for 8% of the time, Pallas kernels for 17%

profile of v3, /device:TPU:16, one launch (start us, length us, event | category | flops | bytes accessed | tf_op | source)
XLA Modules:
  0.0 121.3 jit_solution(14835151836533975100)
XLA Ops:
  0.0 2.9 %spread.1 = bf16[8,272,256]{2,1,0:T(8,128)(2,1)} custom-call(bf16[4,32,4096]{2,1,0:T(8,128)(2,1)} %c_hbm.1, s32[4,32]{1,0:T(4,128)} %go_hbm.1, s32[4,32]{1,0:T(4,128)} %gv_hbm.1, s32[4,32]{1,0:T(4,128)} %mask_hbm.1), custom_call_target="tpu_custom_call" | custom-call | tf_op jit(solution)/shard_map/spread/pallas_call | solution.py:147
  2.9 8.5 %all-to-all-start = ((bf16[8,272,256]{2,1,0:T(8,128)(2,1)}), bf16[8,272,256]{2,1,0:T(8,128)(2,1)S(1)}, u32[]{:S(2)}, u32[]{:S(2)}) async-start(bf16[8,272,256]{2,1,0:T(8,128)(2,1)} %spread.1), calls=%async_computation | async-start | bytes 2228224 | tf_op jit(solution)/shard_map/all_to_all | solution.py:161
  11.4 0.9 constant_dynamic-slice_fusion
  12.3 2.8 %collective-permute-start.2 = (bf16[32,4096]{1,0:T(8,128)(2,1)}, bf16[32,4096]{1,0:T(8,128)(2,1)}, u32[]{:S(2)}, u32[]{:S(2)}) collective-permute-start(bf16[32,4096]{1,0:T(8,128)(2,1)} %get-tuple-element.7), channel_id=1, source_target_pairs={{0,48},{16,0},{32,16},{48,32},{1,49},{17,1},{33,17},{49,33},{2,50}... | collective-permute-start | bytes 786440 | tf_op jit(solution)/shard_map/ppermute | solution.py:167
  15.1 0.8 collective-permute-start.1
  15.9 0.9 collective-permute-start
  16.8 2.2 %copy.8 = bf16[64,64,64]{0,2,1:T(8,128)(2,1)S(1)} copy(bf16[64,64,64]{2,1,0:T(8,128)(2,1)} %param.7) | data formatting | bytes 1048576 | tf_op args[1]
  19.7 2.4 %copy.10.gt_ref = bf16[64,64,64]{2,1,0:T(8,128)(2,1)} copy(bf16[64,64,64]{0,2,1:T(8,128)(2,1)S(1)} %bitcast.24) | data formatting | bytes 1048576 | tf_op jit(solution)/shard_map/reshape | solution.py:174
  22.9 3.5 %collective-permute-done.2 = bf16[32,4096]{1,0:T(8,128)(2,1)} collective-permute-done((bf16[32,4096]{1,0:T(8,128)(2,1)}, bf16[32,4096]{1,0:T(8,128)(2,1)}, u32[]{:S(2)}, u32[]{:S(2)}) %collective-permute-start.2) | collective-permute-done | bytes 262176 | tf_op jit(solution)/shard_map/ppermute | solution.py:167
  26.3 3.7 %collective-permute-done = bf16[32,4096]{1,0:T(8,128)(2,1)} collective-permute-done((bf16[32,4096]{1,0:T(8,128)(2,1)}, bf16[32,4096]{1,0:T(8,128)(2,1)}, u32[]{:S(2)}, u32[]{:S(2)}) %collective-permute-start) | collective-permute-done | bytes 262176 | tf_op jit(solution)/shard_map/ppermute | solution.py:167
  30.0 2.2 %pad_maximum_fusion.refs_0_ = bf16[4,32,4096]{2,1,0:T(8,128)(2,1)} fusion(bf16[1,32,4096]{2,1,0:T(8,128)(2,1)} %bitcast.14, bf16[1,32,4096]{2,1,0:T(8,128)(2,1)} %bitcast.12, bf16[1,32,4096]{2,1,0:T(8,128)(2,1)} %bitcast.10, bf16[1,32,4096]{2,1,0:T(8,128)(2,1)S(1)} %get-tuple-element.5), kind=kLoop, calls=%fused_computation.5 | loop fusion | flops 1572864 | bytes 2097152 | tf_op jit(solution)/shard_map/stack | solution.py:168
  32.2 1.3 %collective-permute-start.4 = (bf16[4,32,4096]{2,1,0:T(8,128)(2,1)}, bf16[4,32,4096]{2,1,0:T(8,128)(2,1)}, u32[]{:S(2)}, u32[]{:S(2)}) collective-permute-start(bf16[4,32,4096]{2,1,0:T(8,128)(2,1)} %pad_maximum_fusion.refs_0_), channel_id=1, source_target_pairs={{0,64},{64,128},{128,192},{192,0},{1,65},{65,129},{129,193},{193,1... | collective-permute-start | bytes 3145736 | tf_op jit(solution)/shard_map/ppermute | solution.py:171
  34.2 1.5 %collective-permute-start.8 = (bf16[4,32,4096]{2,1,0:T(8,128)(2,1)}, bf16[4,32,4096]{2,1,0:T(8,128)(2,1)}, u32[]{:S(2)}, u32[]{:S(2)}) collective-permute-start(bf16[4,32,4096]{2,1,0:T(8,128)(2,1)} %pad_maximum_fusion.refs_0_), channel_id=1, source_target_pairs={{0,128},{64,192},{128,0},{192,64},{1,129},{65,193},{129,1},{193,65... | collective-permute-start | bytes 3145736 | tf_op jit(solution)/shard_map/ppermute | solution.py:171
  35.8 5.8 %all-to-all-done.w_ref = bf16[8,272,256]{2,1,0:T(8,128)(2,1)S(1)} async-done(((bf16[8,272,256]{2,1,0:T(8,128)(2,1)}), bf16[8,272,256]{2,1,0:T(8,128)(2,1)S(1)}, u32[]{:S(2)}, u32[]{:S(2)}) %all-to-all-start) | async-done | bytes 1114144 | tf_op jit(solution)/shard_map/all_to_all | solution.py:161
  41.6 1.2 %copy-done.1 = bf16[64,64,64]{2,1,0:T(8,128)(2,1)S(1)} copy-done((bf16[64,64,64]{2,1,0:T(8,128)(2,1)S(1)}, bf16[64,64,64]{2,1,0:T(8,128)(2,1)}, u32[]{:S(2)}) %copy-start.1) | copy-done | bytes 524312
  42.8 20.8 %image.1 = bf16[4,8,4,4096]{3,2,1,0:T(4,128)(2,1)S(1)} custom-call(s32[32,32]{1,0:T(8,128)S(1)} %bitcast.23, s32[32,32]{1,0:T(8,128)S(1)} %bitcast.22, bf16[8,272,256]{2,1,0:T(8,128)(2,1)S(1)} %all-to-all-done.w_ref, bf16[64,64,64]{2,1,0:T(8,128)(2,1)S(1)} %copy-done.1, bf16[65,128,128]{2,1,0:T(8,128)(2,1)S(1)} %concatenate.15.vb_ref), custom_call_target="tpu_custom_call" | custom-call | tf_op jit(solution)/shard_map/image/pallas_call | solution.py:184
  63.7 1.0 copy-done
  64.6 4.7 %all-to-all-start.1 = ((bf16[32,4,4096]{2,1,0:T(4,128)(2,1)}), bf16[32,4,4096]{2,1,0:T(4,128)(2,1)S(1)}, u32[]{:S(2)}, u32[]{:S(2)}) async-start(bf16[32,4,4096]{2,1,0:T(4,128)(2,1)} %bitcast.20), calls=%async_computation.1 | async-start | bytes 2097152 | tf_op jit(solution)/shard_map/all_to_all | solution.py:197
  69.4 10.7 %collective-permute-done.4.refs_2_ = bf16[4,32,4096]{2,1,0:T(8,128)(2,1)} collective-permute-done((bf16[4,32,4096]{2,1,0:T(8,128)(2,1)}, bf16[4,32,4096]{2,1,0:T(8,128)(2,1)}, u32[]{:S(2)}, u32[]{:S(2)}) %collective-permute-start.4) | collective-permute-done | bytes 1048608 | tf_op jit(solution)/shard_map/ppermute | solution.py:171
  80.8 3.6 %collective-permute-done.5.refs_3_ = bf16[4,32,4096]{2,1,0:T(8,128)(2,1)S(1)} collective-permute-done((bf16[4,32,4096]{2,1,0:T(8,128)(2,1)}, bf16[4,32,4096]{2,1,0:T(8,128)(2,1)S(1)}, u32[]{:S(2)}, u32[]{:S(2)}) %collective-permute-start.5) | collective-permute-done | bytes 1048608 | tf_op jit(solution)/shard_map/ppermute | solution.py:172
  84.6 1.5 %collective-permute-done.9.refs_7_ = bf16[4,32,4096]{2,1,0:T(8,128)(2,1)} collective-permute-done((bf16[4,32,4096]{2,1,0:T(8,128)(2,1)}, bf16[4,32,4096]{2,1,0:T(8,128)(2,1)}, u32[]{:S(2)}, u32[]{:S(2)}) %collective-permute-start.9) | collective-permute-done | bytes 1048608 | tf_op jit(solution)/shard_map/ppermute | solution.py:172
  86.1 12.0 %all-to-all-done.1.im_ref = bf16[32,4,4096]{2,1,0:T(4,128)(2,1)S(1)} async-done(((bf16[32,4,4096]{2,1,0:T(4,128)(2,1)}), bf16[32,4,4096]{2,1,0:T(4,128)(2,1)S(1)}, u32[]{:S(2)}, u32[]{:S(2)}) %all-to-all-start.1) | async-done | bytes 1048608 | tf_op jit(solution)/shard_map/all_to_all | solution.py:197
  98.1 5.8 %chi.1 = bf16[4,8,32,128]{3,2,1,0:T(8,128)(2,1)S(1)} custom-call(s32[3]{0:T(128)S(1)} %pad_add_fusion.pos, bf16[32,4,4096]{2,1,0:T(4,128)(2,1)S(1)} %all-to-all-done.1.im_ref, bf16[4,32,4096]{2,1,0:T(8,128)(2,1)} %pad_maximum_fusion.refs_0_, bf16[4,32,4096]{2,1,0:T(8,128)(2,1)S(1)} %collective-permute-done.3.refs_1_, ...), custom_call_target="tpu_custom_call" | custom-call | tf_op jit(solution)/shard_map/chi/pallas_call | solution.py:199
  103.9 16.7 %all_to_all.15 = bf16[32,32,128]{2,1,0:T(8,128)(2,1)S(1)} all-to-all(bf16[32,32,128]{2,1,0:T(8,128)(2,1)S(1)} %bitcast.21), channel_id=1, replica_groups=mesh['y'=4,'x'=4,'core'=2,'z'=8] {'x','z'}, dimensions={0} | all-to-all | bytes 524288 | tf_op jit(solution)/shard_map/all_to_all | solution.py:208
  (23 shorter events, 3.9 us)
Async XLA Ops:
  0.0 11.4 %copy-start.2 = (bf16[4,32,4096]{2,1,0:T(8,128)(2,1)S(1)}, bf16[4,32,4096]{2,1,0:T(8,128)(2,1)}, u32[]{:S(2)}) copy-start(bf16[4,32,4096]{2,1,0:T(8,128)(2,1)} %c_hbm.1) | copy-start | bytes 3145732
  2.9 38.7 %all-to-all-start = ((bf16[8,272,256]{2,1,0:T(8,128)(2,1)}), bf16[8,272,256]{2,1,0:T(8,128)(2,1)S(1)}, u32[]{:S(2)}, u32[]{:S(2)}) async-start(bf16[8,272,256]{2,1,0:T(8,128)(2,1)} %spread.1), calls=%async_computation | async-start | bytes 2228224 | tf_op jit(solution)/shard_map/all_to_all | solution.py:161
  12.3 14.0 %collective-permute-start.2 = (bf16[32,4096]{1,0:T(8,128)(2,1)}, bf16[32,4096]{1,0:T(8,128)(2,1)}, u32[]{:S(2)}, u32[]{:S(2)}) collective-permute-start(bf16[32,4096]{1,0:T(8,128)(2,1)} %get-tuple-element.7), channel_id=1, source_target_pairs={{0,48},{16,0},{32,16},{48,32},{1,49},{17,1},{33,17},{49,33},{2,50}... | collective-permute-start | bytes 786440 | tf_op jit(solution)/shard_map/ppermute | solution.py:167
  15.1 11.3 %collective-permute-start.1 = (bf16[32,4096]{1,0:T(8,128)(2,1)}, bf16[32,4096]{1,0:T(8,128)(2,1)}, u32[]{:S(2)}, u32[]{:S(2)}) collective-permute-start(bf16[32,4096]{1,0:T(8,128)(2,1)} %get-tuple-element.8), channel_id=1, source_target_pairs={{0,32},{16,48},{32,0},{48,16},{1,33},{17,49},{33,1},{49,17},{2,34}... | collective-permute-start | bytes 786440 | tf_op jit(solution)/shard_map/ppermute | solution.py:167
  15.9 14.1 %collective-permute-start = (bf16[32,4096]{1,0:T(8,128)(2,1)}, bf16[32,4096]{1,0:T(8,128)(2,1)}, u32[]{:S(2)}, u32[]{:S(2)}) collective-permute-start(bf16[32,4096]{1,0:T(8,128)(2,1)} %get-tuple-element.6), channel_id=1, source_target_pairs={{0,16},{16,32},{32,48},{48,0},{1,17},{17,33},{33,49},{49,1},{2,18}... | collective-permute-start | bytes 786440 | tf_op jit(solution)/shard_map/ppermute | solution.py:167
  19.7 2.4 %copy-start.3 = (bf16[64,64,64]{2,1,0:T(8,128)(2,1)S(1)}, bf16[64,64,64]{2,1,0:T(8,128)(2,1)}, u32[]{:S(2)}) copy-start(bf16[64,64,64]{2,1,0:T(8,128)(2,1)} %param.8) | copy-start | bytes 1572868
  32.2 47.9 %collective-permute-start.4 = (bf16[4,32,4096]{2,1,0:T(8,128)(2,1)}, bf16[4,32,4096]{2,1,0:T(8,128)(2,1)}, u32[]{:S(2)}, u32[]{:S(2)}) collective-permute-start(bf16[4,32,4096]{2,1,0:T(8,128)(2,1)} %pad_maximum_fusion.refs_0_), channel_id=1, source_target_pairs={{0,64},{64,128},{128,192},{192,0},{1,65},{65,129},{129,193},{193,1... | collective-permute-start | bytes 3145736 | tf_op jit(solution)/shard_map/ppermute | solution.py:171
  33.5 46.6 %collective-permute-start.6 = (bf16[4,32,4096]{2,1,0:T(8,128)(2,1)}, bf16[4,32,4096]{2,1,0:T(8,128)(2,1)}, u32[]{:S(2)}, u32[]{:S(2)}) collective-permute-start(bf16[4,32,4096]{2,1,0:T(8,128)(2,1)} %pad_maximum_fusion.refs_0_), channel_id=1, source_target_pairs={{0,192},{64,0},{128,64},{192,128},{1,193},{65,1},{129,65},{193,129... | collective-permute-start | bytes 3145736 | tf_op jit(solution)/shard_map/ppermute | solution.py:171
  34.2 46.4 %collective-permute-start.8 = (bf16[4,32,4096]{2,1,0:T(8,128)(2,1)}, bf16[4,32,4096]{2,1,0:T(8,128)(2,1)}, u32[]{:S(2)}, u32[]{:S(2)}) collective-permute-start(bf16[4,32,4096]{2,1,0:T(8,128)(2,1)} %pad_maximum_fusion.refs_0_), channel_id=1, source_target_pairs={{0,128},{64,192},{128,0},{192,64},{1,129},{65,193},{129,1},{193,65... | collective-permute-start | bytes 3145736 | tf_op jit(solution)/shard_map/ppermute | solution.py:171
  41.6 1.2 %copy-start.1 = (bf16[64,64,64]{2,1,0:T(8,128)(2,1)S(1)}, bf16[64,64,64]{2,1,0:T(8,128)(2,1)}, u32[]{:S(2)}) copy-start(bf16[64,64,64]{2,1,0:T(8,128)(2,1)} %copy.10.gt_ref) | copy-start | bytes 1572868
  63.7 1.0 copy-start
  64.6 33.5 %all-to-all-start.1 = ((bf16[32,4,4096]{2,1,0:T(4,128)(2,1)}), bf16[32,4,4096]{2,1,0:T(4,128)(2,1)S(1)}, u32[]{:S(2)}, u32[]{:S(2)}) async-start(bf16[32,4,4096]{2,1,0:T(4,128)(2,1)} %bitcast.20), calls=%async_computation.1 | async-start | bytes 2097152 | tf_op jit(solution)/shard_map/all_to_all | solution.py:197
  69.3 11.4 %collective-permute-start.3 = (bf16[4,32,4096]{2,1,0:T(8,128)(2,1)}, bf16[4,32,4096]{2,1,0:T(8,128)(2,1)S(1)}, u32[]{:S(2)}, u32[]{:S(2)}) collective-permute-start(bf16[4,32,4096]{2,1,0:T(8,128)(2,1)} %pad_maximum_fusion.refs_0_), channel_id=1, source_target_pairs={{0,8},{8,0},{1,9},{9,1},{2,10},{10,2},{3,11},{11,3},{4,12},{12,4},... | collective-permute-start | bytes 3145736 | tf_op jit(solution)/shard_map/ppermute | solution.py:172
  80.1 4.3 %collective-permute-start.5 = (bf16[4,32,4096]{2,1,0:T(8,128)(2,1)}, bf16[4,32,4096]{2,1,0:T(8,128)(2,1)S(1)}, u32[]{:S(2)}, u32[]{:S(2)}) collective-permute-start(bf16[4,32,4096]{2,1,0:T(8,128)(2,1)} %collective-permute-done.4.refs_2_), channel_id=1, source_target_pairs={{0,8},{8,0},{1,9},{9,1},{2,10},{10,2},{3,11},{11,3},{4,12},{12,4},... | collective-permute-start | bytes 3145736 | tf_op jit(solution)/shard_map/ppermute | solution.py:172
  80.1 4.5 %collective-permute-start.7 = (bf16[4,32,4096]{2,1,0:T(8,128)(2,1)}, bf16[4,32,4096]{2,1,0:T(8,128)(2,1)}, u32[]{:S(2)}, u32[]{:S(2)}) collective-permute-start(bf16[4,32,4096]{2,1,0:T(8,128)(2,1)} %collective-permute-done.6.refs_4_), channel_id=1, source_target_pairs={{0,8},{8,0},{1,9},{9,1},{2,10},{10,2},{3,11},{11,3},{4,12},{12,4},... | collective-permute-start | bytes 3145736 | tf_op jit(solution)/shard_map/ppermute | solution.py:172
  80.6 5.5 %collective-permute-start.9 = (bf16[4,32,4096]{2,1,0:T(8,128)(2,1)}, bf16[4,32,4096]{2,1,0:T(8,128)(2,1)}, u32[]{:S(2)}, u32[]{:S(2)}) collective-permute-start(bf16[4,32,4096]{2,1,0:T(8,128)(2,1)} %collective-permute-done.8.refs_6_), channel_id=1, source_target_pairs={{0,8},{8,0},{1,9},{9,1},{2,10},{10,2},{3,11},{11,3},{4,12},{12,4},... | collective-permute-start | bytes 3145736 | tf_op jit(solution)/shard_map/ppermute | solution.py:172

commit v4 on v3

--- a/solution.py
+++ b/solution.py
@@ -62,7 +62,7 @@
     nsrc = w_ref.shape[0]
     pairs = out_ref.shape[1]
     number = nsrc * pairs
-    step, batch = 16, 4
+    step, batch = 16, 2
 
     def finish(zd):
         for kk in range(pairs):
@@ -191,7 +191,7 @@
             VMEM((pairs, 4, width // LANES, LANES), jnp.float32),
             pltpu.SemaphoreType.DMA((nz,)),
         ],
-        compiler_params=pltpu.CompilerParams(vmem_limit_bytes=24 << 20),
+        compiler_params=pltpu.CompilerParams(vmem_limit_bytes=60 << 20),
         name="image",
     )(go_code, gv_code, w, gt, vb)
     image = lax.all_to_all(image.reshape(nx * nz, 4, width), ("x", "z"), 0, 0, tiled=True)

time: 122 us -> 123 us (level)
  Pallas kernels: 29.5 us -> 31 us
    unnamed x9 -> x7, local copies, waits for them, and re-layouts: 4.39 us -> 1.24 us
    all_to_all x1, waiting for transfers between devices: 12 us -> 14 us  [local(): lax.all_to_all(image.reshape(nx * nz, 4, width), ('x', 'z'), 0, 0, tiled=...]
    ppermute x3, waiting for transfers between devices: 10.7 us -> 8.66 us  [local(): lax.ppermute(cx, 'y', [(i, (i + s) % 4) for i in range(4)])]
    pallas_call x1, Pallas kernels: 20.8 us -> 22.4 us  [local(): pl.pallas_call(image_kernel, out_shape=jax.ShapeDtypeStruct((nx, nz, 4, w...]
    concatenate x1, local copies, waits for them, and re-layouts: 0.17 us -> 1.6 us  [local(): jnp.concatenate([vb, jnp.zeros((1, LANES, LANES), jnp.bfloat16)], axis=0)]
  transfers between devices with their start and end apart: 12 -> 12, of which waited for: 8 -> 8; matrix products, arithmetic and copies ran while one was open for 8% -> 8% of each run, Pallas kernels for 17% -> 18%
where the time goes in v4:
time: 123 us; the launch traced here: 122 us
  waiting for transfers between devices  41.5 us (34%)
  Pallas kernels  31 us (25%)
  starting transfers between devices  22.1 us (18%)
  blocking collectives  16.7 us (14%)
  local copies, waits for them, and re-layouts  7.39 us (6%)
  other arithmetic  3.32 us (3%)
    pallas_call x1, Pallas kernels, local(): pl.pallas_call(image_kernel, out_shape=jax.ShapeDtypeStruct((nx, nz, 4, w...  22.4 us
    all_to_all x1, blocking collectives, local(): lax.all_to_all(part.reshape(nx * nz, aux, 4 * aux), ('x', 'z'), 0, 0, til...  16.7 us
    all_to_all x1, waiting for transfers between devices, local(): lax.all_to_all(image.reshape(nx * nz, 4, width), ('x', 'z'), 0, 0, tiled=...  14 us
    ppermute x3, waiting for transfers between devices, local(): lax.ppermute(cx, 'y', [(i, (i + s) % 4) for i in range(4)])  8.66 us
    all_to_all x1, starting transfers between devices, local(): w = lax.all_to_all(spread, 'z', 0, 0, tiled=True)  8.61 us
    all_to_all x1, waiting for transfers between devices, local(): w = lax.all_to_all(spread, 'z', 0, 0, tiled=True)  6.78 us
    ppermute x3, waiting for transfers between devices, local(): lax.ppermute(piece, 'x', [(i, (i + s) % nx) for i in range(nx)])  6.72 us
    pallas_call x1, Pallas kernels, local(): pl.pallas_call(functools.partial(chi_kernel, scale), out_shape=jax.ShapeD...  5.79 us
  transfers between devices with their start and end apart: 12, of which 8 were waited for; matrix products, arithmetic and copies ran while one was open for 8% of the time, Pallas kernels for 18%

profile of v4, /device:TPU:16, one launch (start us, length us, event | category | flops | bytes accessed | tf_op | source)
XLA Modules:
  0.0 122.2 jit_solution(14437055132100370455)
XLA Ops:
  0.0 2.9 %spread.1 = bf16[8,272,256]{2,1,0:T(8,128)(2,1)} custom-call(bf16[4,32,4096]{2,1,0:T(8,128)(2,1)} %c_hbm.1, s32[4,32]{1,0:T(4,128)} %go_hbm.1, s32[4,32]{1,0:T(4,128)} %gv_hbm.1, s32[4,32]{1,0:T(4,128)} %mask_hbm.1), custom_call_target="tpu_custom_call" | custom-call | tf_op jit(solution)/shard_map/spread/pallas_call | solution.py:147
  2.9 8.6 %all-to-all-start = ((bf16[8,272,256]{2,1,0:T(8,128)(2,1)}), bf16[8,272,256]{2,1,0:T(8,128)(2,1)}, u32[]{:S(2)}, u32[]{:S(2)}) async-start(bf16[8,272,256]{2,1,0:T(8,128)(2,1)} %spread.1), calls=%async_computation | async-start | bytes 2228224 | tf_op jit(solution)/shard_map/all_to_all | solution.py:161
  11.5 0.9 constant_dynamic-slice_fusion
  12.4 2.8 %collective-permute-start.2 = (bf16[32,4096]{1,0:T(8,128)(2,1)}, bf16[32,4096]{1,0:T(8,128)(2,1)}, u32[]{:S(2)}, u32[]{:S(2)}) collective-permute-start(bf16[32,4096]{1,0:T(8,128)(2,1)} %get-tuple-element.7), channel_id=1, source_target_pairs={{0,48},{16,0},{32,16},{48,32},{1,49},{17,1},{33,17},{49,33},{2,50}... | collective-permute-start | bytes 786440 | tf_op jit(solution)/shard_map/ppermute | solution.py:167
  15.2 0.8 collective-permute-start.1
  16.0 0.9 collective-permute-start
  16.9 1.2 copy.8
  18.8 2.3 %copy.10.gt_ref = bf16[64,64,64]{2,1,0:T(8,128)(2,1)} copy(bf16[64,64,64]{0,2,1:T(8,128)(2,1)S(1)} %bitcast.21) | data formatting | bytes 1048576 | tf_op jit(solution)/shard_map/reshape | solution.py:174
  21.8 1.6 %concatenate.15.vb_ref = bf16[65,128,128]{2,1,0:T(8,128)(2,1)} pad(bf16[64,128,128]{2,1,0:T(8,128)(2,1)S(1)} %fusion.2, bf16[]{:T(256)} %constant.40.clone.1), padding=0_1x0_0x0_0 | pad | bytes 4227074 | tf_op jit(solution)/shard_map/concatenate | solution.py:179
  23.4 3.1 %collective-permute-done.2 = bf16[32,4096]{1,0:T(8,128)(2,1)} collective-permute-done((bf16[32,4096]{1,0:T(8,128)(2,1)}, bf16[32,4096]{1,0:T(8,128)(2,1)}, u32[]{:S(2)}, u32[]{:S(2)}) %collective-permute-start.2) | collective-permute-done | bytes 262176 | tf_op jit(solution)/shard_map/ppermute | solution.py:167
  26.4 3.7 %collective-permute-done = bf16[32,4096]{1,0:T(8,128)(2,1)} collective-permute-done((bf16[32,4096]{1,0:T(8,128)(2,1)}, bf16[32,4096]{1,0:T(8,128)(2,1)}, u32[]{:S(2)}, u32[]{:S(2)}) %collective-permute-start) | collective-permute-done | bytes 262176 | tf_op jit(solution)/shard_map/ppermute | solution.py:167
  30.1 1.2 %pad_maximum_fusion.refs_0_ = bf16[4,32,4096]{2,1,0:T(8,128)(2,1)S(1)} fusion(bf16[1,32,4096]{2,1,0:T(8,128)(2,1)} %bitcast.14, bf16[1,32,4096]{2,1,0:T(8,128)(2,1)} %bitcast.12, bf16[1,32,4096]{2,1,0:T(8,128)(2,1)} %bitcast.10, bf16[1,32,4096]{2,1,0:T(8,128)(2,1)S(1)} %get-tuple-element.5), kind=kLoop, calls=%fused_computation.5 | loop fusion | flops 1572864 | bytes 2097152 | tf_op jit(solution)/shard_map/stack | solution.py:168
  31.4 1.4 %collective-permute-start.4 = (bf16[4,32,4096]{2,1,0:T(8,128)(2,1)S(1)}, bf16[4,32,4096]{2,1,0:T(8,128)(2,1)S(1)}, u32[]{:S(2)}, u32[]{:S(2)}) collective-permute-start(bf16[4,32,4096]{2,1,0:T(8,128)(2,1)S(1)} %pad_maximum_fusion.refs_0_), channel_id=1, source_target_pairs={{0,64},{64,128},{128,192},{192,0},{1,65},{65,129},{129,193},{193,1... | collective-permute-start | bytes 3145736 | tf_op jit(solution)/shard_map/ppermute | solution.py:171
  32.7 0.7 collective-permute-start.6
  33.5 1.5 %collective-permute-start.8 = (bf16[4,32,4096]{2,1,0:T(8,128)(2,1)S(1)}, bf16[4,32,4096]{2,1,0:T(8,128)(2,1)}, u32[]{:S(2)}, u32[]{:S(2)}) collective-permute-start(bf16[4,32,4096]{2,1,0:T(8,128)(2,1)S(1)} %pad_maximum_fusion.refs_0_), channel_id=1, source_target_pairs={{0,128},{64,192},{128,0},{192,64},{1,129},{65,193},{129,1},{193,65... | collective-permute-start | bytes 3145736 | tf_op jit(solution)/shard_map/ppermute | solution.py:171
  35.0 6.8 %all-to-all-done.w_ref = bf16[8,272,256]{2,1,0:T(8,128)(2,1)} async-done(((bf16[8,272,256]{2,1,0:T(8,128)(2,1)}), bf16[8,272,256]{2,1,0:T(8,128)(2,1)}, u32[]{:S(2)}, u32[]{:S(2)}) %all-to-all-start) | async-done | bytes 1114144 | tf_op jit(solution)/shard_map/all_to_all | solution.py:161
  43.1 22.4 %image.1 = bf16[4,8,4,4096]{3,2,1,0:T(4,128)(2,1)} custom-call(s32[32,32]{1,0:T(8,128)} %bitcast.25, s32[32,32]{1,0:T(8,128)} %bitcast.24, bf16[8,272,256]{2,1,0:T(8,128)(2,1)} %all-to-all-done.w_ref, bf16[64,64,64]{2,1,0:T(8,128)(2,1)} %copy.10.gt_ref, bf16[65,128,128]{2,1,0:T(8,128)(2,1)} %concatenate.15.vb_ref), custom_call_target="tpu_custom_call" | custom-call | tf_op jit(solution)/shard_map/image/pallas_call | solution.py:184
  65.5 4.7 %all-to-all-start.1 = ((bf16[32,4,4096]{2,1,0:T(4,128)(2,1)}), bf16[32,4,4096]{2,1,0:T(4,128)(2,1)S(1)}, u32[]{:S(2)}, u32[]{:S(2)}) async-start(bf16[32,4,4096]{2,1,0:T(4,128)(2,1)} %bitcast.23), calls=%async_computation.1 | async-start | bytes 2097152 | tf_op jit(solution)/shard_map/all_to_all | solution.py:197
  70.3 8.7 %collective-permute-done.4.refs_2_ = bf16[4,32,4096]{2,1,0:T(8,128)(2,1)S(1)} collective-permute-done((bf16[4,32,4096]{2,1,0:T(8,128)(2,1)S(1)}, bf16[4,32,4096]{2,1,0:T(8,128)(2,1)S(1)}, u32[]{:S(2)}, u32[]{:S(2)}) %collective-permute-start.4) | collective-permute-done | bytes 1048608 | tf_op jit(solution)/shard_map/ppermute | solution.py:171
  79.7 3.5 %collective-permute-done.5.refs_3_ = bf16[4,32,4096]{2,1,0:T(8,128)(2,1)} collective-permute-done((bf16[4,32,4096]{2,1,0:T(8,128)(2,1)S(1)}, bf16[4,32,4096]{2,1,0:T(8,128)(2,1)}, u32[]{:S(2)}, u32[]{:S(2)}) %collective-permute-start.5) | collective-permute-done | bytes 1048608 | tf_op jit(solution)/shard_map/ppermute | solution.py:172
  83.5 1.5 %collective-permute-done.9.refs_7_ = bf16[4,32,4096]{2,1,0:T(8,128)(2,1)} collective-permute-done((bf16[4,32,4096]{2,1,0:T(8,128)(2,1)}, bf16[4,32,4096]{2,1,0:T(8,128)(2,1)}, u32[]{:S(2)}, u32[]{:S(2)}) %collective-permute-start.9) | collective-permute-done | bytes 1048608 | tf_op jit(solution)/shard_map/ppermute | solution.py:172
  85.0 14.0 %all-to-all-done.1.im_ref = bf16[32,4,4096]{2,1,0:T(4,128)(2,1)S(1)} async-done(((bf16[32,4,4096]{2,1,0:T(4,128)(2,1)}), bf16[32,4,4096]{2,1,0:T(4,128)(2,1)S(1)}, u32[]{:S(2)}, u32[]{:S(2)}) %all-to-all-start.1) | async-done | bytes 1048608 | tf_op jit(solution)/shard_map/all_to_all | solution.py:197
  99.0 5.8 %chi.1 = bf16[4,8,32,128]{3,2,1,0:T(8,128)(2,1)S(1)} custom-call(s32[3]{0:T(128)S(1)} %pad_add_fusion.pos, bf16[32,4,4096]{2,1,0:T(4,128)(2,1)S(1)} %all-to-all-done.1.im_ref, bf16[4,32,4096]{2,1,0:T(8,128)(2,1)S(1)} %pad_maximum_fusion.refs_0_, bf16[4,32,4096]{2,1,0:T(8,128)(2,1)} %collective-permute-done.3.refs_1_, ...), custom_call_target="tpu_custom_call" | custom-call | tf_op jit(solution)/shard_map/chi/pallas_call | solution.py:199
  104.8 16.7 %all_to_all.15 = bf16[32,32,128]{2,1,0:T(8,128)(2,1)S(1)} all-to-all(bf16[32,32,128]{2,1,0:T(8,128)(2,1)S(1)} %bitcast.20), channel_id=1, replica_groups=mesh['y'=4,'x'=4,'core'=2,'z'=8] {'x','z'}, dimensions={0} | all-to-all | bytes 524288 | tf_op jit(solution)/shard_map/all_to_all | solution.py:208
  (21 shorter events, 4.4 us)
Async XLA Ops:
  0.0 11.5 %copy-start = (bf16[4,32,4096]{2,1,0:T(8,128)(2,1)S(1)}, bf16[4,32,4096]{2,1,0:T(8,128)(2,1)}, u32[]{:S(2)}) copy-start(bf16[4,32,4096]{2,1,0:T(8,128)(2,1)} %c_hbm.1) | copy-start | bytes 3145732
  2.9 14.0 %copy-start.2 = (bf16[64,64,64]{2,1,0:T(8,128)(2,1)S(1)}, bf16[64,64,64]{2,1,0:T(8,128)(2,1)}, u32[]{:S(2)}) copy-start(bf16[64,64,64]{2,1,0:T(8,128)(2,1)} %param.7) | copy-start | bytes 1572868
  2.9 38.9 %all-to-all-start = ((bf16[8,272,256]{2,1,0:T(8,128)(2,1)}), bf16[8,272,256]{2,1,0:T(8,128)(2,1)}, u32[]{:S(2)}, u32[]{:S(2)}) async-start(bf16[8,272,256]{2,1,0:T(8,128)(2,1)} %spread.1), calls=%async_computation | async-start | bytes 2228224 | tf_op jit(solution)/shard_map/all_to_all | solution.py:161
  12.4 14.0 %collective-permute-start.2 = (bf16[32,4096]{1,0:T(8,128)(2,1)}, bf16[32,4096]{1,0:T(8,128)(2,1)}, u32[]{:S(2)}, u32[]{:S(2)}) collective-permute-start(bf16[32,4096]{1,0:T(8,128)(2,1)} %get-tuple-element.7), channel_id=1, source_target_pairs={{0,48},{16,0},{32,16},{48,32},{1,49},{17,1},{33,17},{49,33},{2,50}... | collective-permute-start | bytes 786440 | tf_op jit(solution)/shard_map/ppermute | solution.py:167
  15.2 11.3 %collective-permute-start.1 = (bf16[32,4096]{1,0:T(8,128)(2,1)}, bf16[32,4096]{1,0:T(8,128)(2,1)}, u32[]{:S(2)}, u32[]{:S(2)}) collective-permute-start(bf16[32,4096]{1,0:T(8,128)(2,1)} %get-tuple-element.8), channel_id=1, source_target_pairs={{0,32},{16,48},{32,0},{48,16},{1,33},{17,49},{33,1},{49,17},{2,34}... | collective-permute-start | bytes 786440 | tf_op jit(solution)/shard_map/ppermute | solution.py:167
  16.0 14.1 %collective-permute-start = (bf16[32,4096]{1,0:T(8,128)(2,1)}, bf16[32,4096]{1,0:T(8,128)(2,1)}, u32[]{:S(2)}, u32[]{:S(2)}) collective-permute-start(bf16[32,4096]{1,0:T(8,128)(2,1)} %get-tuple-element.6), channel_id=1, source_target_pairs={{0,16},{16,32},{32,48},{48,0},{1,17},{17,33},{33,49},{49,1},{2,18}... | collective-permute-start | bytes 786440 | tf_op jit(solution)/shard_map/ppermute | solution.py:167
  18.1 3.0 %copy-start.1 = (bf16[64,64,64]{2,1,0:T(8,128)(2,1)S(1)}, bf16[64,64,64]{2,1,0:T(8,128)(2,1)}, u32[]{:S(2)}) copy-start(bf16[64,64,64]{2,1,0:T(8,128)(2,1)} %param.8) | copy-start | bytes 1572868
  31.4 47.6 %collective-permute-start.4 = (bf16[4,32,4096]{2,1,0:T(8,128)(2,1)S(1)}, bf16[4,32,4096]{2,1,0:T(8,128)(2,1)S(1)}, u32[]{:S(2)}, u32[]{:S(2)}) collective-permute-start(bf16[4,32,4096]{2,1,0:T(8,128)(2,1)S(1)} %pad_maximum_fusion.refs_0_), channel_id=1, source_target_pairs={{0,64},{64,128},{128,192},{192,0},{1,65},{65,129},{129,193},{193,1... | collective-permute-start | bytes 3145736 | tf_op jit(solution)/shard_map/ppermute | solution.py:171
  32.7 46.3 %collective-permute-start.6 = (bf16[4,32,4096]{2,1,0:T(8,128)(2,1)S(1)}, bf16[4,32,4096]{2,1,0:T(8,128)(2,1)}, u32[]{:S(2)}, u32[]{:S(2)}) collective-permute-start(bf16[4,32,4096]{2,1,0:T(8,128)(2,1)S(1)} %pad_maximum_fusion.refs_0_), channel_id=1, source_target_pairs={{0,192},{64,0},{128,64},{192,128},{1,193},{65,1},{129,65},{193,129... | collective-permute-start | bytes 3145736 | tf_op jit(solution)/shard_map/ppermute | solution.py:171
  33.5 46.0 %collective-permute-start.8 = (bf16[4,32,4096]{2,1,0:T(8,128)(2,1)S(1)}, bf16[4,32,4096]{2,1,0:T(8,128)(2,1)}, u32[]{:S(2)}, u32[]{:S(2)}) collective-permute-start(bf16[4,32,4096]{2,1,0:T(8,128)(2,1)S(1)} %pad_maximum_fusion.refs_0_), channel_id=1, source_target_pairs={{0,128},{64,192},{128,0},{192,64},{1,129},{65,193},{129,1},{193,65... | collective-permute-start | bytes 3145736 | tf_op jit(solution)/shard_map/ppermute | solution.py:171
  65.5 33.5 %all-to-all-start.1 = ((bf16[32,4,4096]{2,1,0:T(4,128)(2,1)}), bf16[32,4,4096]{2,1,0:T(4,128)(2,1)S(1)}, u32[]{:S(2)}, u32[]{:S(2)}) async-start(bf16[32,4,4096]{2,1,0:T(4,128)(2,1)} %bitcast.23), calls=%async_computation.1 | async-start | bytes 2097152 | tf_op jit(solution)/shard_map/all_to_all | solution.py:197
  70.2 9.4 %collective-permute-start.3 = (bf16[4,32,4096]{2,1,0:T(8,128)(2,1)S(1)}, bf16[4,32,4096]{2,1,0:T(8,128)(2,1)}, u32[]{:S(2)}, u32[]{:S(2)}) collective-permute-start(bf16[4,32,4096]{2,1,0:T(8,128)(2,1)S(1)} %pad_maximum_fusion.refs_0_), channel_id=1, source_target_pairs={{0,8},{8,0},{1,9},{9,1},{2,10},{10,2},{3,11},{11,3},{4,12},{12,4},... | collective-permute-start | bytes 3145736 | tf_op jit(solution)/shard_map/ppermute | solution.py:172
  79.0 4.2 %collective-permute-start.5 = (bf16[4,32,4096]{2,1,0:T(8,128)(2,1)S(1)}, bf16[4,32,4096]{2,1,0:T(8,128)(2,1)}, u32[]{:S(2)}, u32[]{:S(2)}) collective-permute-start(bf16[4,32,4096]{2,1,0:T(8,128)(2,1)S(1)} %collective-permute-done.4.refs_2_), channel_id=1, source_target_pairs={{0,8},{8,0},{1,9},{9,1},{2,10},{10,2},{3,11},{11,3},{4,12},{12,4},... | collective-permute-start | bytes 3145736 | tf_op jit(solution)/shard_map/ppermute | solution.py:172
  79.0 4.5 %collective-permute-start.7 = (bf16[4,32,4096]{2,1,0:T(8,128)(2,1)}, bf16[4,32,4096]{2,1,0:T(8,128)(2,1)}, u32[]{:S(2)}, u32[]{:S(2)}) collective-permute-start(bf16[4,32,4096]{2,1,0:T(8,128)(2,1)} %collective-permute-done.6.refs_4_), channel_id=1, source_target_pairs={{0,8},{8,0},{1,9},{9,1},{2,10},{10,2},{3,11},{11,3},{4,12},{12,4},... | collective-permute-start | bytes 3145736 | tf_op jit(solution)/shard_map/ppermute | solution.py:172
  79.5 5.5 %collective-permute-start.9 = (bf16[4,32,4096]{2,1,0:T(8,128)(2,1)}, bf16[4,32,4096]{2,1,0:T(8,128)(2,1)}, u32[]{:S(2)}, u32[]{:S(2)}) collective-permute-start(bf16[4,32,4096]{2,1,0:T(8,128)(2,1)} %collective-permute-done.8.refs_6_), channel_id=1, source_target_pairs={{0,8},{8,0},{1,9},{9,1},{2,10},{10,2},{3,11},{11,3},{4,12},{12,4},... | collective-permute-start | bytes 3145736 | tf_op jit(solution)/shard_map/ppermute | solution.py:172

commit v5 on v4

--- a/solution.py
+++ b/solution.py
@@ -191,7 +191,7 @@
             VMEM((pairs, 4, width // LANES, LANES), jnp.float32),
             pltpu.SemaphoreType.DMA((nz,)),
         ],
-        compiler_params=pltpu.CompilerParams(vmem_limit_bytes=60 << 20),
+        compiler_params=pltpu.CompilerParams(vmem_limit_bytes=24 << 20),
         name="image",
     )(go_code, gv_code, w, gt, vb)
     image = lax.all_to_all(image.reshape(nx * nz, 4, width), ("x", "z"), 0, 0, tiled=True)

time: 123 us -> 122 us (level)
  Pallas kernels: 31 us -> 29.5 us
    unnamed x7 -> x9, local copies, waits for them, and re-layouts: 1.24 us -> 4.39 us
    ppermute x3, waiting for transfers between devices: 8.66 us -> 10.7 us  [local(): lax.ppermute(cx, 'y', [(i, (i + s) % 4) for i in range(4)])]
    all_to_all x1, waiting for transfers between devices: 14 us -> 12 us  [local(): lax.all_to_all(image.reshape(nx * nz, 4, width), ('x', 'z'), 0, 0, tiled=...]
    pallas_call x1, Pallas kernels: 22.4 us -> 20.8 us  [local(): pl.pallas_call(image_kernel, out_shape=jax.ShapeDtypeStruct((nx, nz, 4, w...]
    concatenate x1, local copies, waits for them, and re-layouts: 1.6 us -> 0.17 us  [local(): jnp.concatenate([vb, jnp.zeros((1, LANES, LANES), jnp.bfloat16)], axis=0)]
  transfers between devices with their start and end apart: 12 -> 12, of which waited for: 8 -> 8; matrix products, arithmetic and copies ran while one was open for 8% -> 8% of each run, Pallas kernels for 18% -> 17%
where the time goes in v5:
time: 122 us; the launch traced here: 121 us
  waiting for transfers between devices  40.9 us (34%)
  Pallas kernels  29.5 us (24%)
  starting transfers between devices  21.9 us (18%)
  blocking collectives  16.7 us (14%)
  local copies, waits for them, and re-layouts  8.58 us (7%)
  other arithmetic  3.58 us (3%)
    pallas_call x1, Pallas kernels, local(): pl.pallas_call(image_kernel, out_shape=jax.ShapeDtypeStruct((nx, nz, 4, w...  20.8 us
    all_to_all x1, blocking collectives, local(): lax.all_to_all(part.reshape(nx * nz, aux, 4 * aux), ('x', 'z'), 0, 0, til...  16.7 us
    all_to_all x1, waiting for transfers between devices, local(): lax.all_to_all(image.reshape(nx * nz, 4, width), ('x', 'z'), 0, 0, tiled=...  12 us
    ppermute x3, waiting for transfers between devices, local(): lax.ppermute(cx, 'y', [(i, (i + s) % 4) for i in range(4)])  10.7 us
    all_to_all x1, starting transfers between devices, local(): w = lax.all_to_all(spread, 'z', 0, 0, tiled=True)  8.48 us
    ppermute x3, waiting for transfers between devices, local(): lax.ppermute(piece, 'x', [(i, (i + s) % nx) for i in range(nx)])  7.13 us
    pallas_call x1, Pallas kernels, local(): pl.pallas_call(functools.partial(chi_kernel, scale), out_shape=jax.ShapeD...  5.8 us
    all_to_all x1, waiting for transfers between devices, local(): w = lax.all_to_all(spread, 'z', 0, 0, tiled=True)  5.76 us
  transfers between devices with their start and end apart: 12, of which 8 were waited for; matrix products, arithmetic and copies ran while one was open for 8% of the time, Pallas kernels for 17%

profile of v5, /device:TPU:16, one launch (start us, length us, event | category | flops | bytes accessed | tf_op | source)
XLA Modules:
  0.0 121.2 jit_solution(9780030097573656440)
XLA Ops:
  0.0 2.9 %spread.1 = bf16[8,272,256]{2,1,0:T(8,128)(2,1)} custom-call(bf16[4,32,4096]{2,1,0:T(8,128)(2,1)} %c_hbm.1, s32[4,32]{1,0:T(4,128)} %go_hbm.1, s32[4,32]{1,0:T(4,128)} %gv_hbm.1, s32[4,32]{1,0:T(4,128)} %mask_hbm.1), custom_call_target="tpu_custom_call" | custom-call | tf_op jit(solution)/shard_map/spread/pallas_call | solution.py:147
  2.9 8.5 %all-to-all-start = ((bf16[8,272,256]{2,1,0:T(8,128)(2,1)}), bf16[8,272,256]{2,1,0:T(8,128)(2,1)S(1)}, u32[]{:S(2)}, u32[]{:S(2)}) async-start(bf16[8,272,256]{2,1,0:T(8,128)(2,1)} %spread.1), calls=%async_computation | async-start | bytes 2228224 | tf_op jit(solution)/shard_map/all_to_all | solution.py:161
  11.4 0.9 constant_dynamic-slice_fusion
  12.3 2.8 %collective-permute-start.2 = (bf16[32,4096]{1,0:T(8,128)(2,1)}, bf16[32,4096]{1,0:T(8,128)(2,1)}, u32[]{:S(2)}, u32[]{:S(2)}) collective-permute-start(bf16[32,4096]{1,0:T(8,128)(2,1)} %get-tuple-element.7), channel_id=1, source_target_pairs={{0,48},{16,0},{32,16},{48,32},{1,49},{17,1},{33,17},{49,33},{2,50}... | collective-permute-start | bytes 786440 | tf_op jit(solution)/shard_map/ppermute | solution.py:167
  15.1 0.8 collective-permute-start.1
  15.9 0.9 collective-permute-start
  16.8 2.2 %copy.8 = bf16[64,64,64]{0,2,1:T(8,128)(2,1)S(1)} copy(bf16[64,64,64]{2,1,0:T(8,128)(2,1)} %param.7) | data formatting | bytes 1048576 | tf_op args[1]
  19.7 2.4 %copy.10.gt_ref = bf16[64,64,64]{2,1,0:T(8,128)(2,1)} copy(bf16[64,64,64]{0,2,1:T(8,128)(2,1)S(1)} %bitcast.24) | data formatting | bytes 1048576 | tf_op jit(solution)/shard_map/reshape | solution.py:174
  22.9 3.5 %collective-permute-done.2 = bf16[32,4096]{1,0:T(8,128)(2,1)} collective-permute-done((bf16[32,4096]{1,0:T(8,128)(2,1)}, bf16[32,4096]{1,0:T(8,128)(2,1)}, u32[]{:S(2)}, u32[]{:S(2)}) %collective-permute-start.2) | collective-permute-done | bytes 262176 | tf_op jit(solution)/shard_map/ppermute | solution.py:167
  26.3 3.7 %collective-permute-done = bf16[32,4096]{1,0:T(8,128)(2,1)} collective-permute-done((bf16[32,4096]{1,0:T(8,128)(2,1)}, bf16[32,4096]{1,0:T(8,128)(2,1)}, u32[]{:S(2)}, u32[]{:S(2)}) %collective-permute-start) | collective-permute-done | bytes 262176 | tf_op jit(solution)/shard_map/ppermute | solution.py:167
  30.0 2.2 %pad_maximum_fusion.refs_0_ = bf16[4,32,4096]{2,1,0:T(8,128)(2,1)} fusion(bf16[1,32,4096]{2,1,0:T(8,128)(2,1)} %bitcast.14, bf16[1,32,4096]{2,1,0:T(8,128)(2,1)} %bitcast.12, bf16[1,32,4096]{2,1,0:T(8,128)(2,1)} %bitcast.10, bf16[1,32,4096]{2,1,0:T(8,128)(2,1)S(1)} %get-tuple-element.5), kind=kLoop, calls=%fused_computation.5 | loop fusion | flops 1572864 | bytes 2097152 | tf_op jit(solution)/shard_map/stack | solution.py:168
  32.2 1.3 %collective-permute-start.4 = (bf16[4,32,4096]{2,1,0:T(8,128)(2,1)}, bf16[4,32,4096]{2,1,0:T(8,128)(2,1)}, u32[]{:S(2)}, u32[]{:S(2)}) collective-permute-start(bf16[4,32,4096]{2,1,0:T(8,128)(2,1)} %pad_maximum_fusion.refs_0_), channel_id=1, source_target_pairs={{0,64},{64,128},{128,192},{192,0},{1,65},{65,129},{129,193},{193,1... | collective-permute-start | bytes 3145736 | tf_op jit(solution)/shard_map/ppermute | solution.py:171
  34.2 1.5 %collective-permute-start.8 = (bf16[4,32,4096]{2,1,0:T(8,128)(2,1)}, bf16[4,32,4096]{2,1,0:T(8,128)(2,1)}, u32[]{:S(2)}, u32[]{:S(2)}) collective-permute-start(bf16[4,32,4096]{2,1,0:T(8,128)(2,1)} %pad_maximum_fusion.refs_0_), channel_id=1, source_target_pairs={{0,128},{64,192},{128,0},{192,64},{1,129},{65,193},{129,1},{193,65... | collective-permute-start | bytes 3145736 | tf_op jit(solution)/shard_map/ppermute | solution.py:171
  35.8 5.8 %all-to-all-done.w_ref = bf16[8,272,256]{2,1,0:T(8,128)(2,1)S(1)} async-done(((bf16[8,272,256]{2,1,0:T(8,128)(2,1)}), bf16[8,272,256]{2,1,0:T(8,128)(2,1)S(1)}, u32[]{:S(2)}, u32[]{:S(2)}) %all-to-all-start) | async-done | bytes 1114144 | tf_op jit(solution)/shard_map/all_to_all | solution.py:161
  41.6 1.2 %copy-done.1 = bf16[64,64,64]{2,1,0:T(8,128)(2,1)S(1)} copy-done((bf16[64,64,64]{2,1,0:T(8,128)(2,1)S(1)}, bf16[64,64,64]{2,1,0:T(8,128)(2,1)}, u32[]{:S(2)}) %copy-start.1) | copy-done | bytes 524312
  42.8 20.8 %image.1 = bf16[4,8,4,4096]{3,2,1,0:T(4,128)(2,1)S(1)} custom-call(s32[32,32]{1,0:T(8,128)S(1)} %bitcast.23, s32[32,32]{1,0:T(8,128)S(1)} %bitcast.22, bf16[8,272,256]{2,1,0:T(8,128)(2,1)S(1)} %all-to-all-done.w_ref, bf16[64,64,64]{2,1,0:T(8,128)(2,1)S(1)} %copy-done.1, bf16[65,128,128]{2,1,0:T(8,128)(2,1)S(1)} %concatenate.15.vb_ref), custom_call_target="tpu_custom_call" | custom-call | tf_op jit(solution)/shard_map/image/pallas_call | solution.py:184
  63.6 1.0 copy-done
  64.6 4.7 %all-to-all-start.1 = ((bf16[32,4,4096]{2,1,0:T(4,128)(2,1)}), bf16[32,4,4096]{2,1,0:T(4,128)(2,1)S(1)}, u32[]{:S(2)}, u32[]{:S(2)}) async-start(bf16[32,4,4096]{2,1,0:T(4,128)(2,1)} %bitcast.20), calls=%async_computation.1 | async-start | bytes 2097152 | tf_op jit(solution)/shard_map/all_to_all | solution.py:197
  69.4 10.7 %collective-permute-done.4.refs_2_ = bf16[4,32,4096]{2,1,0:T(8,128)(2,1)} collective-permute-done((bf16[4,32,4096]{2,1,0:T(8,128)(2,1)}, bf16[4,32,4096]{2,1,0:T(8,128)(2,1)}, u32[]{:S(2)}, u32[]{:S(2)}) %collective-permute-start.4) | collective-permute-done | bytes 1048608 | tf_op jit(solution)/shard_map/ppermute | solution.py:171
  80.8 3.6 %collective-permute-done.5.refs_3_ = bf16[4,32,4096]{2,1,0:T(8,128)(2,1)S(1)} collective-permute-done((bf16[4,32,4096]{2,1,0:T(8,128)(2,1)}, bf16[4,32,4096]{2,1,0:T(8,128)(2,1)S(1)}, u32[]{:S(2)}, u32[]{:S(2)}) %collective-permute-start.5) | collective-permute-done | bytes 1048608 | tf_op jit(solution)/shard_map/ppermute | solution.py:172
  84.6 1.5 %collective-permute-done.9.refs_7_ = bf16[4,32,4096]{2,1,0:T(8,128)(2,1)} collective-permute-done((bf16[4,32,4096]{2,1,0:T(8,128)(2,1)}, bf16[4,32,4096]{2,1,0:T(8,128)(2,1)}, u32[]{:S(2)}, u32[]{:S(2)}) %collective-permute-start.9) | collective-permute-done | bytes 1048608 | tf_op jit(solution)/shard_map/ppermute | solution.py:172
  86.1 12.0 %all-to-all-done.1.im_ref = bf16[32,4,4096]{2,1,0:T(4,128)(2,1)S(1)} async-done(((bf16[32,4,4096]{2,1,0:T(4,128)(2,1)}), bf16[32,4,4096]{2,1,0:T(4,128)(2,1)S(1)}, u32[]{:S(2)}, u32[]{:S(2)}) %all-to-all-start.1) | async-done | bytes 1048608 | tf_op jit(solution)/shard_map/all_to_all | solution.py:197
  98.1 5.8 %chi.1 = bf16[4,8,32,128]{3,2,1,0:T(8,128)(2,1)S(1)} custom-call(s32[3]{0:T(128)S(1)} %pad_add_fusion.pos, bf16[32,4,4096]{2,1,0:T(4,128)(2,1)S(1)} %all-to-all-done.1.im_ref, bf16[4,32,4096]{2,1,0:T(8,128)(2,1)} %pad_maximum_fusion.refs_0_, bf16[4,32,4096]{2,1,0:T(8,128)(2,1)S(1)} %collective-permute-done.3.refs_1_, ...), custom_call_target="tpu_custom_call" | custom-call | tf_op jit(solution)/shard_map/chi/pallas_call | solution.py:199
  103.9 16.7 %all_to_all.15 = bf16[32,32,128]{2,1,0:T(8,128)(2,1)S(1)} all-to-all(bf16[32,32,128]{2,1,0:T(8,128)(2,1)S(1)} %bitcast.21), channel_id=1, replica_groups=mesh['y'=4,'x'=4,'core'=2,'z'=8] {'x','z'}, dimensions={0} | all-to-all | bytes 524288 | tf_op jit(solution)/shard_map/all_to_all | solution.py:208
  (23 shorter events, 3.9 us)
Async XLA Ops:
  0.0 11.4 %copy-start.2 = (bf16[4,32,4096]{2,1,0:T(8,128)(2,1)S(1)}, bf16[4,32,4096]{2,1,0:T(8,128)(2,1)}, u32[]{:S(2)}) copy-start(bf16[4,32,4096]{2,1,0:T(8,128)(2,1)} %c_hbm.1) | copy-start | bytes 3145732
  2.9 38.7 %all-to-all-start = ((bf16[8,272,256]{2,1,0:T(8,128)(2,1)}), bf16[8,272,256]{2,1,0:T(8,128)(2,1)S(1)}, u32[]{:S(2)}, u32[]{:S(2)}) async-start(bf16[8,272,256]{2,1,0:T(8,128)(2,1)} %spread.1), calls=%async_computation | async-start | bytes 2228224 | tf_op jit(solution)/shard_map/all_to_all | solution.py:161
  12.3 14.0 %collective-permute-start.2 = (bf16[32,4096]{1,0:T(8,128)(2,1)}, bf16[32,4096]{1,0:T(8,128)(2,1)}, u32[]{:S(2)}, u32[]{:S(2)}) collective-permute-start(bf16[32,4096]{1,0:T(8,128)(2,1)} %get-tuple-element.7), channel_id=1, source_target_pairs={{0,48},{16,0},{32,16},{48,32},{1,49},{17,1},{33,17},{49,33},{2,50}... | collective-permute-start | bytes 786440 | tf_op jit(solution)/shard_map/ppermute | solution.py:167
  15.1 11.3 %collective-permute-start.1 = (bf16[32,4096]{1,0:T(8,128)(2,1)}, bf16[32,4096]{1,0:T(8,128)(2,1)}, u32[]{:S(2)}, u32[]{:S(2)}) collective-permute-start(bf16[32,4096]{1,0:T(8,128)(2,1)} %get-tuple-element.8), channel_id=1, source_target_pairs={{0,32},{16,48},{32,0},{48,16},{1,33},{17,49},{33,1},{49,17},{2,34}... | collective-permute-start | bytes 786440 | tf_op jit(solution)/shard_map/ppermute | solution.py:167
  15.9 14.1 %collective-permute-start = (bf16[32,4096]{1,0:T(8,128)(2,1)}, bf16[32,4096]{1,0:T(8,128)(2,1)}, u32[]{:S(2)}, u32[]{:S(2)}) collective-permute-start(bf16[32,4096]{1,0:T(8,128)(2,1)} %get-tuple-element.6), channel_id=1, source_target_pairs={{0,16},{16,32},{32,48},{48,0},{1,17},{17,33},{33,49},{49,1},{2,18}... | collective-permute-start | bytes 786440 | tf_op jit(solution)/shard_map/ppermute | solution.py:167
  19.7 2.4 %copy-start.3 = (bf16[64,64,64]{2,1,0:T(8,128)(2,1)S(1)}, bf16[64,64,64]{2,1,0:T(8,128)(2,1)}, u32[]{:S(2)}) copy-start(bf16[64,64,64]{2,1,0:T(8,128)(2,1)} %param.8) | copy-start | bytes 1572868
  32.2 47.9 %collective-permute-start.4 = (bf16[4,32,4096]{2,1,0:T(8,128)(2,1)}, bf16[4,32,4096]{2,1,0:T(8,128)(2,1)}, u32[]{:S(2)}, u32[]{:S(2)}) collective-permute-start(bf16[4,32,4096]{2,1,0:T(8,128)(2,1)} %pad_maximum_fusion.refs_0_), channel_id=1, source_target_pairs={{0,64},{64,128},{128,192},{192,0},{1,65},{65,129},{129,193},{193,1... | collective-permute-start | bytes 3145736 | tf_op jit(solution)/shard_map/ppermute | solution.py:171
  33.5 46.6 %collective-permute-start.6 = (bf16[4,32,4096]{2,1,0:T(8,128)(2,1)}, bf16[4,32,4096]{2,1,0:T(8,128)(2,1)}, u32[]{:S(2)}, u32[]{:S(2)}) collective-permute-start(bf16[4,32,4096]{2,1,0:T(8,128)(2,1)} %pad_maximum_fusion.refs_0_), channel_id=1, source_target_pairs={{0,192},{64,0},{128,64},{192,128},{1,193},{65,1},{129,65},{193,129... | collective-permute-start | bytes 3145736 | tf_op jit(solution)/shard_map/ppermute | solution.py:171
  34.2 46.4 %collective-permute-start.8 = (bf16[4,32,4096]{2,1,0:T(8,128)(2,1)}, bf16[4,32,4096]{2,1,0:T(8,128)(2,1)}, u32[]{:S(2)}, u32[]{:S(2)}) collective-permute-start(bf16[4,32,4096]{2,1,0:T(8,128)(2,1)} %pad_maximum_fusion.refs_0_), channel_id=1, source_target_pairs={{0,128},{64,192},{128,0},{192,64},{1,129},{65,193},{129,1},{193,65... | collective-permute-start | bytes 3145736 | tf_op jit(solution)/shard_map/ppermute | solution.py:171
  41.6 1.2 %copy-start.1 = (bf16[64,64,64]{2,1,0:T(8,128)(2,1)S(1)}, bf16[64,64,64]{2,1,0:T(8,128)(2,1)}, u32[]{:S(2)}) copy-start(bf16[64,64,64]{2,1,0:T(8,128)(2,1)} %copy.10.gt_ref) | copy-start | bytes 1572868
  63.6 1.0 copy-start
  64.6 33.5 %all-to-all-start.1 = ((bf16[32,4,4096]{2,1,0:T(4,128)(2,1)}), bf16[32,4,4096]{2,1,0:T(4,128)(2,1)S(1)}, u32[]{:S(2)}, u32[]{:S(2)}) async-start(bf16[32,4,4096]{2,1,0:T(4,128)(2,1)} %bitcast.20), calls=%async_computation.1 | async-start | bytes 2097152 | tf_op jit(solution)/shard_map/all_to_all | solution.py:197
  69.3 11.5 %collective-permute-start.3 = (bf16[4,32,4096]{2,1,0:T(8,128)(2,1)}, bf16[4,32,4096]{2,1,0:T(8,128)(2,1)S(1)}, u32[]{:S(2)}, u32[]{:S(2)}) collective-permute-start(bf16[4,32,4096]{2,1,0:T(8,128)(2,1)} %pad_maximum_fusion.refs_0_), channel_id=1, source_target_pairs={{0,8},{8,0},{1,9},{9,1},{2,10},{10,2},{3,11},{11,3},{4,12},{12,4},... | collective-permute-start | bytes 3145736 | tf_op jit(solution)/shard_map/ppermute | solution.py:172
  80.1 4.3 %collective-permute-start.5 = (bf16[4,32,4096]{2,1,0:T(8,128)(2,1)}, bf16[4,32,4096]{2,1,0:T(8,128)(2,1)S(1)}, u32[]{:S(2)}, u32[]{:S(2)}) collective-permute-start(bf16[4,32,4096]{2,1,0:T(8,128)(2,1)} %collective-permute-done.4.refs_2_), channel_id=1, source_target_pairs={{0,8},{8,0},{1,9},{9,1},{2,10},{10,2},{3,11},{11,3},{4,12},{12,4},... | collective-permute-start | bytes 3145736 | tf_op jit(solution)/shard_map/ppermute | solution.py:172
  80.1 4.5 %collective-permute-start.7 = (bf16[4,32,4096]{2,1,0:T(8,128)(2,1)}, bf16[4,32,4096]{2,1,0:T(8,128)(2,1)}, u32[]{:S(2)}, u32[]{:S(2)}) collective-permute-start(bf16[4,32,4096]{2,1,0:T(8,128)(2,1)} %collective-permute-done.6.refs_4_), channel_id=1, source_target_pairs={{0,8},{8,0},{1,9},{9,1},{2,10},{10,2},{3,11},{11,3},{4,12},{12,4},... | collective-permute-start | bytes 3145736 | tf_op jit(solution)/shard_map/ppermute | solution.py:172
  80.6 5.5 %collective-permute-start.9 = (bf16[4,32,4096]{2,1,0:T(8,128)(2,1)}, bf16[4,32,4096]{2,1,0:T(8,128)(2,1)}, u32[]{:S(2)}, u32[]{:S(2)}) collective-permute-start(bf16[4,32,4096]{2,1,0:T(8,128)(2,1)} %collective-permute-done.8.refs_6_), channel_id=1, source_target_pairs={{0,8},{8,0},{1,9},{9,1},{2,10},{10,2},{3,11},{11,3},{4,12},{12,4},... | collective-permute-start | bytes 3145736 | tf_op jit(solution)/shard_map/ppermute | solution.py:172
